TPU v7x, 512 devices: a whole 4x8x8 slice. The times are simulated.
512 devices in a mesh: rows: 128 (over z, y, core), band: 4 (over x).
Axes of the slice: x: 4, y: 8, z: 8, core: 2. Of those that a mesh axis runs over, the one named last changes fastest.
Arguments:
- frames: bfloat16 [2, 512, 512, 96], P(None, 'rows'), may hold values from -6 to 6
- conv_weight: bfloat16 [3, 3, 96, 128], replicated, may hold values from -0.21875 to 0.21875
- proj_weight: bfloat16 [128, 256], replicated, may hold values from -0.5 to 0.5
- band_start: int32 [128], P('rows'), may hold values from -4 to 4, as said below
- band_count: int32 [128], P('rows'), may hold values from 1 to 8, as said below
- pyramid_grad: bfloat16 [128, 2, 4, 512, 960], P('rows', None, 'band'), may hold values from -6 to 6
Outputs:
- pyramid: bfloat16 [128, 2, 4, 512, 960], P('rows', None, 'band')
- source_grad: float32 [256, 256, 256], P('rows', None, 'band')
- target_grad: float32 [256, 256, 256], P('rows', None, 'band')
Inputs may be any that keep to these rules, and one draw needn't show every extreme that they name: Row block b's band covers target blocks b + band_start[b] to b + band_start[b] + band_count[b] - 1, all within b - 4 to b + 4. `band_count`: some row block's band has 8 target blocks and some other's has 1.
All inputs are finite; a program needn't handle non-finite values.
Results may differ from a plain program's by a relative error of at most 0.0034.
Values may be sent and summed in bfloat16 or wider, within the bound.
A program may use at most 128 MiB of HBM per device.

v0:
```python
import math

import jax
import jax.numpy as jnp
from jax import lax
from jax.sharding import PartitionSpec as P

LEVELS = 4
ROWS_DEV = 2
COLUMNS = 256
BAND_REACH = 4
PIXELS = 512


HIGHEST = lax.Precision.HIGHEST


def shifted(x, axis, by):
    size = lax.axis_size(axis)
    pairs = [(i, i + by) for i in range(size) if 0 <= i + by < size]
    return lax.ppermute(x, axis, pairs)


def convolve(extended, conv_weight, proj_weight):
    convolved = lax.conv_general_dilated(
        extended,
        conv_weight,
        (2, 2),
        ((0, 0), (1, 0)),
        dimension_numbers=("NHWC", "HWIO", "NHWC"),
        preferred_element_type=jnp.float32,
    )
    middle = jax.nn.relu(convolved).astype(jnp.bfloat16)
    batches = middle.shape[0]
    flattened = jnp.dot(
        middle.reshape(-1, middle.shape[3]), proj_weight, preferred_element_type=jnp.float32
    )
    return flattened.reshape(batches, -1, proj_weight.shape[1])


def pool_levels(correlation):
    row_count = correlation.shape[0]
    levels = []
    for level_index in range(LEVELS):
        group_size = 2**level_index
        pooled = correlation.reshape(row_count, ROWS_DEV, COLUMNS // group_size, group_size)
        levels.append(jnp.mean(pooled, axis=3).reshape(row_count, PIXELS // group_size))
    return jnp.concatenate(levels, axis=1)


def spread_levels(gradient):
    row_count = gradient.shape[0]
    summed = gradient[:, :PIXELS]
    column_start = PIXELS
    for level_index in range(1, LEVELS):
        group_size = 2**level_index
        level_width = PIXELS // group_size
        level_part = gradient[:, column_start : column_start + level_width].reshape(
            row_count, ROWS_DEV, level_width // ROWS_DEV, 1
        )
        spread = jnp.broadcast_to(
            level_part / group_size, (row_count, ROWS_DEV, level_width // ROWS_DEV, group_size)
        )
        summed = summed + spread.reshape(row_count, PIXELS)
        column_start = column_start + level_width
    return summed


def add_into(window_grad, window_place, target_part):
    current = lax.dynamic_index_in_dim(window_grad, window_place, 0, keepdims=False)
    return lax.dynamic_update_index_in_dim(window_grad, current + target_part, window_place, 0)


def shards(frames, conv_weight, proj_weight, band_start, band_count, pyramid_grad):
    band_size = lax.axis_size("band")
    position = lax.axis_index("band")
    channels = proj_weight.shape[1]
    share_width = channels // band_size
    factor = 1.0 / math.sqrt(channels)
    rim_row = shifted(frames[:, -1:], "rows", 1)
    extended = jnp.concatenate([rim_row, frames], axis=1)
    features = convolve(extended, conv_weight, proj_weight)
    source = features[0]
    own_target = features[1]
    pieces = []
    for offset in range(-BAND_REACH, BAND_REACH + 1):
        if offset == 0:
            pieces.append(own_target)
        else:
            pieces.append(shifted(own_target, "rows", -offset))
    window = jnp.stack(pieces)
    band_first = band_start[0]
    band_width = band_count[0]
    source_sum = jnp.zeros(source.shape, jnp.float32)
    slot_count = pyramid_grad.shape[1]
    outputs = []
    tile_parts = []
    tile_places = []
    for slot_local in range(slot_count):
        slot_index = slot_local * band_size + position
        window_place = band_first + slot_index + BAND_REACH
        target = lax.dynamic_index_in_dim(window, window_place, 0, keepdims=False)

        def compute(operands):
            source_block, target_block, grad_block = operands
            correlation = (
                lax.dot_general(
                    source_block, target_block, (((1,), (1,)), ((), ())), precision=HIGHEST
                )
                * factor
            )
            pyramid = pool_levels(correlation).astype(jnp.bfloat16)
            grad_corr = spread_levels(grad_block.astype(jnp.float32))
            source_part = jnp.dot(grad_corr, target_block, precision=HIGHEST) * factor
            target_part = (
                lax.dot_general(
                    grad_corr, source_block, (((0,), (0,)), ((), ())), precision=HIGHEST
                )
                * factor
            )
            return (pyramid, source_part, target_part)

        def skipped(operands):
            source_block, target_block, grad_block = operands
            return (
                jnp.zeros(grad_block.shape, jnp.bfloat16),
                jnp.zeros_like(source_block),
                jnp.zeros_like(source_block),
            )

        pyramid, source_part, target_part = lax.cond(
            slot_index < band_width,
            compute,
            skipped,
            (source, target, pyramid_grad[0, slot_local, 0]),
        )
        pyramid, source_part, target_part, window_place = (
            pyramid,
            source_part,
            target_part,
            window_place,
        )
        outputs.append(pyramid)
        source_sum = source_sum + source_part
        tile_parts.append(target_part)
        tile_places.append(window_place)
    pyramid_out = jnp.stack(outputs)[None, :, None]
    shape_out = (ROWS_DEV, COLUMNS, share_width)
    window_grad = jnp.zeros(window.shape, jnp.float32)
    for tile_index in range(len(tile_parts)):
        window_grad = add_into(window_grad, tile_places[tile_index], tile_parts[tile_index])
    received = window_grad[BAND_REACH]
    for offset in range(-BAND_REACH, BAND_REACH + 1):
        if offset != 0:
            received = received + shifted(window_grad[offset + BAND_REACH], "rows", offset)
    source_share, target_share = (
        lax.psum_scatter(source_sum, "band", scatter_dimension=1, tiled=True),
        lax.psum_scatter(received, "band", scatter_dimension=1, tiled=True),
    )
    return (pyramid_out, source_share.reshape(shape_out), target_share.reshape(shape_out))


def solution(mesh):
    in_specs = (
        P(None, "rows", None, None),
        P(),
        P(),
        P("rows"),
        P("rows"),
        P("rows", None, "band", None, None),
    )
    out_specs = (
        P("rows", None, "band", None, None),
        P("rows", None, "band"),
        P("rows", None, "band"),
    )
    return jax.shard_map(shards, mesh=mesh, in_specs=in_specs, out_specs=out_specs, check_vma=False)
```

profile of v0, /device:TPU:1, one launch (start us, length us, event | category | flops | bytes accessed | tf_op | source)
XLA Modules:
  0.0 285.3 jit_solution(14459275076451888600)
XLA Ops:
  8.2 4.6 %collective-permute-start = (bf16[2,1,512,96]{2,3,1,0:T(8,128)(2,1)S(1)}, bf16[2,1,512,96]{2,3,1,0:T(8,128)(2,1)S(1)}, u32[]{:S(2)}, u32[]{:S(2)}) collective-permute-start(bf16[2,1,512,96]{2,3,1,0:T(8,128)(2,1)S(1)} %slice.82), channel_id=1, source_target_pairs={{0,4},{4,8},{8,12},{12,16},{16,20},{20,24},{24,28},{28,32},{32,36}... | collective-permute-start | bytes 589832 | tf_op jit(solution)/shard_map/ppermute | solution.py:21
  12.8 4.5 %collective-permute-done = bf16[2,1,512,96]{2,3,1,0:T(8,128)(2,1)S(1)} collective-permute-done((bf16[2,1,512,96]{2,3,1,0:T(8,128)(2,1)S(1)}, bf16[2,1,512,96]{2,3,1,0:T(8,128)(2,1)S(1)}, u32[]{:S(2)}, u32[]{:S(2)}) %collective-permute-start) | collective-permute-done | bytes 196640 | tf_op jit(solution)/shard_map/ppermute | solution.py:21
  21.0 3.5 %fusion.17 = bf16[5,2,8,68,96]{4,1,3,2,0:T(2,128)(2,1)S(1)} fusion(bf16[5,2,7,2,96]{4,1,3,2,0:T(2,128)(2,1)S(1)} %slice.105, bf16[5,2,8,66,96]{4,1,3,2,0:T(2,128)(2,1)S(1)} %bitcast.173), kind=kLoop, calls=%fused_computation.47 | loop fusion | flops 3133440 | bytes 2085120 | tf_op jit(solution)/shard_map/conv_general_dilated | solution.py:25
  29.3 8.1 %collective-permute-start.2 = (f32[512,256]{1,0:T(8,128)}, f32[512,256]{1,0:T(8,128)S(1)}, u32[]{:S(2)}, u32[]{:S(2)}) collective-permute-start(f32[512,256]{1,0:T(8,128)} %get-tuple-element.96), channel_id=1, source_target_pairs={{0,12},{4,16},{8,20},{12,24},{16,28},{20,32},{24,36},{28,40},{32,4... | collective-permute-start | bytes 1572872 | tf_op jit(solution)/shard_map/ppermute | solution.py:21
  40.1 3.0 %collective-permute-start.4 = (f32[512,256]{1,0:T(8,128)}, f32[512,256]{1,0:T(8,128)S(1)}, u32[]{:S(2)}, u32[]{:S(2)}) collective-permute-start(f32[512,256]{1,0:T(8,128)} %get-tuple-element.96), channel_id=1, source_target_pairs={{0,4},{4,8},{8,12},{12,16},{16,20},{20,24},{24,28},{28,32},{32,36}... | collective-permute-start | bytes 1572872 | tf_op jit(solution)/shard_map/ppermute | solution.py:21
  47.2 16.7 %collective-permute-done.2 = f32[512,256]{1,0:T(8,128)S(1)} collective-permute-done((f32[512,256]{1,0:T(8,128)}, f32[512,256]{1,0:T(8,128)S(1)}, u32[]{:S(2)}, u32[]{:S(2)}) %collective-permute-start.2) | collective-permute-done | bytes 524320 | tf_op jit(solution)/shard_map/ppermute | solution.py:21
  66.1 12.9 %collective-permute-done.3 = f32[512,256]{1,0:T(8,128)S(1)} collective-permute-done((f32[512,256]{1,0:T(8,128)}, f32[512,256]{1,0:T(8,128)S(1)}, u32[]{:S(2)}, u32[]{:S(2)}) %collective-permute-start.3) | collective-permute-done | bytes 524320 | tf_op jit(solution)/shard_map/ppermute | solution.py:21
  81.1 5.2 %collective-permute-done.4 = f32[512,256]{1,0:T(8,128)S(1)} collective-permute-done((f32[512,256]{1,0:T(8,128)}, f32[512,256]{1,0:T(8,128)S(1)}, u32[]{:S(2)}, u32[]{:S(2)}) %collective-permute-start.4) | collective-permute-done | bytes 524320 | tf_op jit(solution)/shard_map/ppermute | solution.py:21
  89.7 16.7 %collective-permute-done.7 = f32[512,256]{1,0:T(8,128)S(1)} collective-permute-done((f32[512,256]{1,0:T(8,128)}, f32[512,256]{1,0:T(8,128)S(1)}, u32[]{:S(2)}, u32[]{:S(2)}) %collective-permute-start.7) | collective-permute-done | bytes 524320 | tf_op jit(solution)/shard_map/ppermute | solution.py:21
  107.2 5.1 %collective-permute-done.8 = f32[512,256]{1,0:T(8,128)S(1)} collective-permute-done((f32[512,256]{1,0:T(8,128)}, f32[512,256]{1,0:T(8,128)S(1)}, u32[]{:S(2)}, u32[]{:S(2)}) %collective-permute-start.8) | collective-permute-done | bytes 524320 | tf_op jit(solution)/shard_map/ppermute | solution.py:21
  113.2 22.3 %conditional.2 = (f32[512,256]{1,0:T(8,128)}, bf16[1,512,960]{1,2,0:T(8,128)(2,1)}, f32[1,512,256]{1,2,0:T(8,128)}) conditional(s32[]{:T(128)} %convert_element_type.37, () %tuple.34, (bf16[1,2,1,512,960]{3,4,2,1,0:T(8,128)(2,1)S(1)}, f32[9,512,256]{2,1,0:T(8,128)}, s32[]{:T(128)}, f32[512,256]{1,0:T(8,128)S(1)}) %tuple.63), branch_computations={%region_0.1_spmd, %region_1.5_spmd} | conditional | flops 2423160832 | bytes 35652640 | solution.py:131
  119.1 3.7 %convolution_multiply_fusion.2 = f32[512,256]{1,0:T(8,128)} fusion(f32[512,512]{0,1:T(8,128)S(1)} %fusion.2, f32[9,512,256]{2,1,0:T(8,128)} %get-tuple-element.46, s32[]{:T(128)} %get-tuple-element.47), kind=kOutput, calls=%fused_computation.3 | convolution fusion | flops 805437440 | bytes 2097664 | tf_op jit(solution)/shard_map/cond/branch_1_fun/dot_general | solution.py:114
  140.3 18.9 %conditional.3 = (f32[512,256]{1,0:T(8,128)S(1)}, f32[512,256]{1,0:T(8,128)}, bf16[1,512,960]{1,2,0:T(8,128)(2,1)}) conditional(s32[]{:T(128)} %convert_element_type.39, () %tuple.36, (bf16[1,2,1,512,960]{3,4,2,1,0:T(8,128)(2,1)}, f32[9,512,256]{2,1,0:T(8,128)}, s32[]{:T(128)}, f32[512,256]{1,0:T(8,128)S(1)}) %tuple.37), branch_computations={%region_5.6_spmd, %region_6.10_spmd} | conditional | flops 2423160832 | bytes 36701244 | solution.py:131
  147.4 3.7 %convolution_multiply_fusion.5 = f32[512,256]{1,0:T(8,128)} fusion(f32[512,512]{0,1:T(8,128)S(1)} %fusion.10, f32[9,512,256]{2,1,0:T(8,128)} %get-tuple-element.50, s32[]{:T(128)} %get-tuple-element.51), kind=kOutput, calls=%fused_computation.25 | convolution fusion | flops 805437440 | bytes 2097664 | tf_op jit(solution)/shard_map/cond/branch_1_fun/dot_general | solution.py:114
  161.5 4.0 %slice_bitcast_fusion.7 = (f32[512,256]{0,1:T(8,128)S(1)}, f32[512,256]{0,1:T(8,128)}, f32[512,256]{0,1:T(8,128)}, f32[512,256]{0,1:T(8,128)}, f32[512,256]{0,1:...) fusion(f32[9,512,256]{1,2,0:T(8,128)} %constant_dynamic-update-slice_fusion), kind=kLoop, calls=%fused_computation.62 | loop fusion | bytes 8388608 | tf_op jit(solution)/shard_map/squeeze | solution.py:155
  176.9 11.3 %collective-permute-done.16 = f32[512,256]{0,1:T(8,128)S(1)} collective-permute-done((f32[512,256]{0,1:T(8,128)}, f32[512,256]{0,1:T(8,128)S(1)}, u32[]{:S(2)}, u32[]{:S(2)}) %collective-permute-start.16) | collective-permute-done | bytes 524320 | tf_op jit(solution)/shard_map/ppermute | solution.py:21
  189.5 12.6 %collective-permute-done.15 = f32[512,256]{0,1:T(8,128)S(1)} collective-permute-done((f32[512,256]{0,1:T(8,128)}, f32[512,256]{0,1:T(8,128)S(1)}, u32[]{:S(2)}, u32[]{:S(2)}) %collective-permute-start.15) | collective-permute-done | bytes 524320 | tf_op jit(solution)/shard_map/ppermute | solution.py:21
  203.4 5.3 %collective-permute-done.14 = f32[512,256]{0,1:T(8,128)} collective-permute-done((f32[512,256]{0,1:T(8,128)}, f32[512,256]{0,1:T(8,128)}, u32[]{:S(2)}, u32[]{:S(2)}) %collective-permute-start.14) | collective-permute-done | bytes 524320 | tf_op jit(solution)/shard_map/ppermute | solution.py:21
  209.9 4.3 %collective-permute-done.13 = f32[512,256]{0,1:T(8,128)S(1)} collective-permute-done((f32[512,256]{0,1:T(8,128)}, f32[512,256]{0,1:T(8,128)S(1)}, u32[]{:S(2)}, u32[]{:S(2)}) %collective-permute-start.13) | collective-permute-done | bytes 524320 | tf_op jit(solution)/shard_map/ppermute | solution.py:21
  214.3 19.9 %collective-permute-done.10 = f32[512,256]{0,1:T(8,128)S(1)} collective-permute-done((f32[512,256]{0,1:T(8,128)S(1)}, f32[512,256]{0,1:T(8,128)S(1)}, u32[]{:S(2)}, u32[]{:S(2)}) %collective-permute-start.10) | collective-permute-done | bytes 524320 | tf_op jit(solution)/shard_map/ppermute | solution.py:21
  234.2 5.1 %collective-permute-done.9 = f32[512,256]{0,1:T(8,128)S(1)} collective-permute-done((f32[512,256]{0,1:T(8,128)S(1)}, f32[512,256]{0,1:T(8,128)S(1)}, u32[]{:S(2)}, u32[]{:S(2)}) %collective-permute-start.9) | collective-permute-done | bytes 524320 | tf_op jit(solution)/shard_map/ppermute | solution.py:21
  239.3 2.6 fusion.37
  241.9 3.0 %maximum_bitcast_fusion = bf16[1,2,1,512,960]{3,4,2,1,0:T(8,128)(2,1)} fusion(bf16[1,512,960]{1,2,0:T(8,128)(2,1)} %get-tuple-element.63, bf16[1,512,960]{1,2,0:T(8,128)(2,1)} %get-tuple-element.62), kind=kLoop, calls=%fused_computation.46 | loop fusion | flops 983040 | bytes 3932160 | tf_op jit(solution)/shard_map/broadcast_in_dim | solution.py:147
  246.7 30.2 %reduce-scatter.5.cloned.1.call-done = f32[512,64]{0,1:T(8,128)} async-done(((f32[512,256]{0,1:T(8,128)}), f32[512,64]{0,1:T(8,128)}) %reduce-scatter.5.cloned.1.call-update) | async-done | bytes 131088 | tf_op jit(solution)/shard_map/reduce_scatter | solution.py:158
  (111 shorter events, 83.4 us)
Async XLA Ops:
  7.2 17.4 %copy-start = (bf16[3,3,96,128]{3,2,1,0:T(8,128)(2,1)S(1)}, bf16[3,3,96,128]{3,2,1,0:T(8,128)(2,1)}, u32[]{:S(2)}) copy-start(bf16[3,3,96,128]{3,2,1,0:T(8,128)(2,1)} %param.11) | copy-start | bytes 663556
  7.2 237.7 %reduce-scatter.7.cloned.1.call-start = ((), (), s32[]{:S(2)}) async-start(), calls=%async_computation.3 | async-start | bytes 655360
  8.2 9.1 %collective-permute-start = (bf16[2,1,512,96]{2,3,1,0:T(8,128)(2,1)S(1)}, bf16[2,1,512,96]{2,3,1,0:T(8,128)(2,1)S(1)}, u32[]{:S(2)}, u32[]{:S(2)}) collective-permute-start(bf16[2,1,512,96]{2,3,1,0:T(8,128)(2,1)S(1)} %slice.82), channel_id=1, source_target_pairs={{0,4},{4,8},{8,12},{12,16},{16,20},{20,24},{24,28},{28,32},{32,36}... | collective-permute-start | bytes 589832 | tf_op jit(solution)/shard_map/ppermute | solution.py:21
  19.6 5.0 %copy-start.6 = (pred[16,33]{0,1:T(8,128)(4,1)S(1)}, pred[16,33]{0,1:T(8,128)(4,1)}, u32[]{:S(2)}) copy-start(pred[16,33]{0,1:T(8,128)(4,1)} %constant.104) | copy-start | bytes 1588
  21.0 4.8 %copy-start.5 = (bf16[128,256]{1,0:T(8,128)(2,1)S(1)}, bf16[128,256]{1,0:T(8,128)(2,1)}, u32[]{:S(2)}) copy-start(bf16[128,256]{1,0:T(8,128)(2,1)} %param.12) | copy-start | bytes 196612
  26.9 18.1 %collective-permute-start.1 = (f32[512,256]{1,0:T(8,128)}, f32[512,256]{1,0:T(8,128)S(1)}, u32[]{:S(2)}, u32[]{:S(2)}) collective-permute-start(f32[512,256]{1,0:T(8,128)} %get-tuple-element.96), channel_id=1, source_target_pairs={{0,16},{4,20},{8,24},{12,28},{16,32},{20,36},{24,40},{28,44},{32,4... | collective-permute-start | bytes 1572872 | tf_op jit(solution)/shard_map/ppermute | solution.py:21
  29.3 34.6 %collective-permute-start.2 = (f32[512,256]{1,0:T(8,128)}, f32[512,256]{1,0:T(8,128)S(1)}, u32[]{:S(2)}, u32[]{:S(2)}) collective-permute-start(f32[512,256]{1,0:T(8,128)} %get-tuple-element.96), channel_id=1, source_target_pairs={{0,12},{4,16},{8,20},{12,24},{16,28},{20,32},{24,36},{28,40},{32,4... | collective-permute-start | bytes 1572872 | tf_op jit(solution)/shard_map/ppermute | solution.py:21
  37.4 41.6 %collective-permute-start.3 = (f32[512,256]{1,0:T(8,128)}, f32[512,256]{1,0:T(8,128)S(1)}, u32[]{:S(2)}, u32[]{:S(2)}) collective-permute-start(f32[512,256]{1,0:T(8,128)} %get-tuple-element.96), channel_id=1, source_target_pairs={{0,8},{4,12},{8,16},{12,20},{16,24},{20,28},{24,32},{28,36},{32,40... | collective-permute-start | bytes 1572872 | tf_op jit(solution)/shard_map/ppermute | solution.py:21
  40.1 46.3 %collective-permute-start.4 = (f32[512,256]{1,0:T(8,128)}, f32[512,256]{1,0:T(8,128)S(1)}, u32[]{:S(2)}, u32[]{:S(2)}) collective-permute-start(f32[512,256]{1,0:T(8,128)} %get-tuple-element.96), channel_id=1, source_target_pairs={{0,4},{4,8},{8,12},{12,16},{16,20},{20,24},{24,28},{28,32},{32,36}... | collective-permute-start | bytes 1572872 | tf_op jit(solution)/shard_map/ppermute | solution.py:21
  43.1 44.9 %collective-permute-start.5 = (f32[512,256]{1,0:T(8,128)}, f32[512,256]{1,0:T(8,128)S(1)}, u32[]{:S(2)}, u32[]{:S(2)}) collective-permute-start(f32[512,256]{1,0:T(8,128)} %get-tuple-element.96), channel_id=1, source_target_pairs={{4,0},{8,4},{12,8},{16,12},{20,16},{24,20},{28,24},{32,28},{36,32}... | collective-permute-start | bytes 1572872 | tf_op jit(solution)/shard_map/ppermute | solution.py:21
  45.0 43.8 %collective-permute-start.6 = (f32[512,256]{1,0:T(8,128)}, f32[512,256]{1,0:T(8,128)S(1)}, u32[]{:S(2)}, u32[]{:S(2)}) collective-permute-start(f32[512,256]{1,0:T(8,128)} %get-tuple-element.96), channel_id=1, source_target_pairs={{8,0},{12,4},{16,8},{20,12},{24,16},{28,20},{32,24},{36,28},{40,32... | collective-permute-start | bytes 1572872 | tf_op jit(solution)/shard_map/ppermute | solution.py:21
  63.9 42.5 %collective-permute-start.7 = (f32[512,256]{1,0:T(8,128)}, f32[512,256]{1,0:T(8,128)S(1)}, u32[]{:S(2)}, u32[]{:S(2)}) collective-permute-start(f32[512,256]{1,0:T(8,128)} %get-tuple-element.96), channel_id=1, source_target_pairs={{12,0},{16,4},{20,8},{24,12},{28,16},{32,20},{36,24},{40,28},{44,3... | collective-permute-start | bytes 1572872 | tf_op jit(solution)/shard_map/ppermute | solution.py:21
  79.0 33.4 %collective-permute-start.8 = (f32[512,256]{1,0:T(8,128)}, f32[512,256]{1,0:T(8,128)S(1)}, u32[]{:S(2)}, u32[]{:S(2)}) collective-permute-start(f32[512,256]{1,0:T(8,128)} %get-tuple-element.96), channel_id=1, source_target_pairs={{16,0},{20,4},{24,8},{28,12},{32,16},{36,20},{40,24},{44,28},{48,3... | collective-permute-start | bytes 1572872 | tf_op jit(solution)/shard_map/ppermute | solution.py:21
  87.2 26.1 %copy-start.4 = (bf16[1,2,1,512,960]{3,4,2,1,0:T(8,128)(2,1)S(1)}, bf16[1,2,1,512,960]{3,4,2,1,0:T(8,128)(2,1)}, u32[]{:S(2)}) copy-start(bf16[1,2,1,512,960]{3,4,2,1,0:T(8,128)(2,1)} %param.15) | copy-start | bytes 5898244
  165.6 22.7 %collective-permute-start.16 = (f32[512,256]{0,1:T(8,128)}, f32[512,256]{0,1:T(8,128)S(1)}, u32[]{:S(2)}, u32[]{:S(2)}) collective-permute-start(f32[512,256]{0,1:T(8,128)} %get-tuple-element.88), channel_id=1, source_target_pairs={{0,16},{4,20},{8,24},{12,28},{16,32},{20,36},{24,40},{28,44},{32,4... | collective-permute-start | bytes 1572872 | tf_op jit(solution)/shard_map/ppermute | solution.py:21
  166.9 35.2 %collective-permute-start.15 = (f32[512,256]{0,1:T(8,128)}, f32[512,256]{0,1:T(8,128)S(1)}, u32[]{:S(2)}, u32[]{:S(2)}) collective-permute-start(f32[512,256]{0,1:T(8,128)} %get-tuple-element.89), channel_id=1, source_target_pairs={{0,12},{4,16},{8,20},{12,24},{16,28},{20,32},{24,36},{28,40},{32,4... | collective-permute-start | bytes 1572872 | tf_op jit(solution)/shard_map/ppermute | solution.py:21
  168.2 40.4 %collective-permute-start.14 = (f32[512,256]{0,1:T(8,128)}, f32[512,256]{0,1:T(8,128)}, u32[]{:S(2)}, u32[]{:S(2)}) collective-permute-start(f32[512,256]{0,1:T(8,128)} %get-tuple-element.90), channel_id=1, source_target_pairs={{0,8},{4,12},{8,16},{12,20},{16,24},{20,28},{24,32},{28,36},{32,40... | collective-permute-start | bytes 1572872 | tf_op jit(solution)/shard_map/ppermute | solution.py:21
  172.5 104.4 %reduce-scatter.5.cloned.1.call-start = ((), (), s32[]{:S(2)}) async-start(), calls=%async_computation.2 | async-start | bytes 655360 | tf_op jit(solution)/shard_map/reduce_scatter | solution.py:158
  172.5 41.7 %collective-permute-start.13 = (f32[512,256]{0,1:T(8,128)}, f32[512,256]{0,1:T(8,128)S(1)}, u32[]{:S(2)}, u32[]{:S(2)}) collective-permute-start(f32[512,256]{0,1:T(8,128)} %get-tuple-element.91), channel_id=1, source_target_pairs={{0,4},{4,8},{8,12},{12,16},{16,20},{20,24},{24,28},{28,32},{32,36}... | collective-permute-start | bytes 1572872 | tf_op jit(solution)/shard_map/ppermute | solution.py:21
  174.5 39.8 %collective-permute-start.12 = (f32[512,256]{0,1:T(8,128)}, f32[512,256]{0,1:T(8,128)S(1)}, u32[]{:S(2)}, u32[]{:S(2)}) collective-permute-start(f32[512,256]{0,1:T(8,128)} %get-tuple-element.92), channel_id=1, source_target_pairs={{4,0},{8,4},{12,8},{16,12},{20,16},{24,20},{28,24},{32,28},{36,32}... | collective-permute-start | bytes 1572872 | tf_op jit(solution)/shard_map/ppermute | solution.py:21
  188.3 26.0 %collective-permute-start.11 = (f32[512,256]{0,1:T(8,128)}, f32[512,256]{0,1:T(8,128)S(1)}, u32[]{:S(2)}, u32[]{:S(2)}) collective-permute-start(f32[512,256]{0,1:T(8,128)} %get-tuple-element.93), channel_id=1, source_target_pairs={{8,0},{12,4},{16,8},{20,12},{24,16},{28,20},{32,24},{36,28},{40,32... | collective-permute-start | bytes 1572872 | tf_op jit(solution)/shard_map/ppermute | solution.py:21
  202.1 32.1 %collective-permute-start.10 = (f32[512,256]{0,1:T(8,128)S(1)}, f32[512,256]{0,1:T(8,128)S(1)}, u32[]{:S(2)}, u32[]{:S(2)}) collective-permute-start(f32[512,256]{0,1:T(8,128)S(1)} %get-tuple-element.94), channel_id=1, source_target_pairs={{12,0},{16,4},{20,8},{24,12},{28,16},{32,20},{36,24},{40,28},{44,3... | collective-permute-start | bytes 1572872 | tf_op jit(solution)/shard_map/ppermute | solution.py:21
  208.7 30.6 %collective-permute-start.9 = (f32[512,256]{0,1:T(8,128)S(1)}, f32[512,256]{0,1:T(8,128)S(1)}, u32[]{:S(2)}, u32[]{:S(2)}) collective-permute-start(f32[512,256]{0,1:T(8,128)S(1)} %get-tuple-element.87), channel_id=1, source_target_pairs={{16,0},{20,4},{24,8},{28,12},{32,16},{36,20},{40,24},{44,28},{48,3... | collective-permute-start | bytes 1572872 | tf_op jit(solution)/shard_map/ppermute | solution.py:21
  239.3 39.2 %copy-start.1 = (bf16[3,3,96,128]{3,2,1,0:T(8,128)(2,1)S(1)}, bf16[3,3,96,128]{3,2,1,0:T(8,128)(2,1)}, u32[]{:S(2)}) copy-start(bf16[3,3,96,128]{3,2,1,0:T(8,128)(2,1)} %param.11) | copy-start | bytes 663556
  (2 other events, 4.5 us)
Sparse Core Ops, SparseCore 0:
  172.6 36.9 reduce-scatter.6
  242.0 34.8 reduce-scatter.4
where the time goes:
time: 288 us; the launch traced here: 285 us
  waiting for transfers between devices  150 us (52%)
  local copies, waits for them, and re-layouts  38.6 us (13%)
  starting transfers between devices  38.2 us (13%)
  other arithmetic  26.9 us (9%)
  matrix products  15.8 us (5%)
  between operations  15.7 us (5%)
    ppermute x17, waiting for transfers between devices, shifted(): return lax.ppermute(x, axis, pairs)  120 us
    ppermute x17, starting transfers between devices, shifted(): return lax.ppermute(x, axis, pairs)  38.2 us
    reduce_scatter x1, waiting for transfers between devices, shards(): lax.psum_scatter(received, 'band', scatter_dimension=1, tiled=True)  30.2 us
    unnamed x24, local copies, waits for them, and re-layouts  12.8 us
    dot_general x2, matrix products, compute(): source_part = jnp.dot(grad_corr, target_block, precision=HIGHEST) * factor  7.38 us
    reduce_sum x4, other arithmetic, pool_levels(): jnp.mean(pooled, axis=3).reshape(row_count, PIXELS // group_size)  6.17 us
    reshape x4, local copies, waits for them, and re-layouts, spread_levels(): summed = summed + spread.reshape(row_count, PIXELS)  6.05 us
  transfers between devices with their start and end apart: 19, of which 13 were waited for; matrix products, arithmetic and copies ran while one was open for 6% of the time, Pallas kernels for 0%

commit v1 on v0

v1 whole, which is shorter than its diff:
```python
import jax
import jax.numpy as jnp
from jax import lax
from jax.experimental import pallas as pl
from jax.experimental.pallas import tpu as pltpu
from jax.sharding import PartitionSpec as P

ROWS_DEV = 2
BAND_REACH = 4
PIXELS = 512
MID = 128
LOWER = 448
BANDS = 4
QUARTER = PIXELS // BANDS
SHARE = 64
SCALE = 1.0 / 16.0
F32 = jnp.float32
BF16 = jnp.bfloat16


def shifted(x, axis, by):
    size = lax.axis_size(axis)
    pairs = [(i, i + by) for i in range(size) if 0 <= i + by < size]
    return lax.ppermute(x, axis, pairs)


def halves(x):
    high = x.astype(BF16)
    return high, (x - high.astype(F32)).astype(BF16)


def dot(a, b, da=1, db=0):
    return lax.dot_general(a, b, (((da,), (db,)), ((), ())), preferred_element_type=F32)


def tile_kernel(count_ref, source_ref, target_ref, grad_ref, proj_ref, pyramid_ref, terms_ref, share_ref, pool, pair, total):
    j = pl.program_id(0)
    source = source_ref[...]

    @pl.when(j == 0)
    def _():
        row = lax.broadcasted_iota(jnp.int32, (LOWER, PIXELS), 0)
        column = lax.broadcasted_iota(jnp.int32, (LOWER, PIXELS), 1)
        shift = jnp.where(row < 256, 1, jnp.where(row < 384, 2, 3))
        first = jnp.where(row < 256, 0, jnp.where(row < 384, 256, 384))
        weight = jnp.where(row < 256, 0.5, jnp.where(row < 384, 0.25, 0.125))
        pool[...] = jnp.where((column >> shift) == row - first, weight, 0.0).astype(BF16)
        square_high, square_low = halves(dot(proj_ref[...], proj_ref[...], 1, 1) * SCALE)
        high, low = halves(dot(source, square_high) + dot(source, square_low))
        pair[...] = jnp.concatenate([high, low], axis=1)

    valid = j * BANDS + lax.axis_index("band") < count_ref[0]
    target = target_ref[0]
    grad = grad_ref[0, 0, 0]
    high, low = halves(dot(pool[...], target))
    base = dot(pair[...], jnp.concatenate([target, target], axis=1), 1, 1)
    rest = dot(pair[...], jnp.concatenate([high, high], axis=1), 1, 1) + dot(pair[:, :MID], low, 1, 1)
    pyramid_ref[0, 0, 0, :, :PIXELS] = jnp.where(valid, base, 0.0).astype(BF16)
    pyramid_ref[0, 0, 0, :, PIXELS:] = jnp.where(valid, rest, 0.0).astype(BF16)
    both = dot(grad[:, PIXELS:], jnp.concatenate([high, low], axis=1))
    part = jnp.where(valid, dot(grad[:, :PIXELS], target) + both[:, :MID] + both[:, MID:], 0.0)
    spread = dot(source, grad, 0, 0)
    high, low = halves(spread[:, PIXELS:])
    term = (spread[:, :PIXELS] + dot(high, pool[...]) + dot(low, pool[...])) * SCALE
    term = jnp.where(valid, term, 0.0).astype(BF16)
    for q in range(BANDS):
        terms_ref[q, 0] = term[:, q * QUARTER : (q + 1) * QUARTER]

    @pl.when(j == 0)
    def _():
        total[...] = part

    @pl.when(j == 1)
    def _():
        high, low = halves((total[...] + part) * SCALE)
        proj = proj_ref[...]
        wide = dot(proj, high, 0, 1) + dot(proj, low, 0, 1)
        for q in range(BANDS):
            share_ref[q] = wide[q * SHARE : (q + 1) * SHARE].astype(BF16)


def tiles(count, source, target, grad, proj):
    return pl.pallas_call(
        tile_kernel,
        grid=(2,),
        in_specs=[
            pl.BlockSpec(memory_space=pltpu.SMEM),
            pl.BlockSpec((PIXELS, MID), lambda j: (0, 0)),
            pl.BlockSpec((1, PIXELS, MID), lambda j: (j, 0, 0)),
            pl.BlockSpec((1, 1, 1, PIXELS, 960), lambda j: (0, j, 0, 0, 0)),
            pl.BlockSpec((MID, 256), lambda j: (0, 0)),
        ],
        out_specs=[
            pl.BlockSpec((1, 1, 1, PIXELS, 960), lambda j: (0, j, 0, 0, 0)),
            pl.BlockSpec((BANDS, 1, MID, QUARTER), lambda j: (0, j, 0, 0)),
            pl.BlockSpec((BANDS, SHARE, PIXELS), lambda j: (0, 0, 0)),
        ],
        out_shape=[
            jax.ShapeDtypeStruct((1, 2, 1, PIXELS, 960), BF16),
            jax.ShapeDtypeStruct((BANDS, 2, MID, QUARTER), BF16),
            jax.ShapeDtypeStruct((BANDS, SHARE, PIXELS), BF16),
        ],
        scratch_shapes=[
            pltpu.VMEM((LOWER, PIXELS), BF16),
            pltpu.VMEM((PIXELS, 2 * MID), BF16),
            pltpu.VMEM((PIXELS, MID), F32),
        ],
    )(count, source, target, grad, proj)


def swap(parts):
    here = lax.axis_index("band")
    got = [lax.dynamic_index_in_dim(parts, here, 0, keepdims=False)]
    for d in range(1, BANDS):
        out = lax.dynamic_index_in_dim(parts, (here + d) % BANDS, 0, keepdims=False)
        got.append(lax.ppermute(out, "band", [(i, (i + d) % BANDS) for i in range(BANDS)]))
    return jnp.stack(got)[(here - jnp.arange(BANDS)) % BANDS]


def shards(frames, conv_weight, proj_weight, band_start, band_count, pyramid_grad):
    here = lax.axis_index("band")
    start = band_start[0]
    rim_row = shifted(frames[:, -1:], "rows", 1)
    convolved = lax.conv_general_dilated(
        jnp.concatenate([rim_row, frames], axis=1),
        conv_weight,
        (2, 2),
        ((0, 0), (1, 0)),
        dimension_numbers=("NHWC", "HWIO", "NHWC"),
        preferred_element_type=F32,
    )
    middle = jax.nn.relu(convolved).astype(BF16).reshape(2, PIXELS, MID)
    own = lax.dynamic_slice_in_dim(middle[1], here * QUARTER, QUARTER, 0)
    offsets = range(-BAND_REACH, BAND_REACH + 1)
    window = jnp.stack([own if o == 0 else shifted(own, "rows", -o) for o in offsets])
    places = start + BAND_REACH + jnp.arange(2)[None] * BANDS + jnp.arange(BANDS)[:, None]
    chosen = window[jnp.clip(places, 0, 2 * BAND_REACH)]
    target = jnp.swapaxes(swap(chosen), 0, 1).reshape(2, PIXELS, MID)
    pyramid, terms, share = tiles(band_count, middle[0], target, pyramid_grad, proj_weight)
    slots = jnp.swapaxes(swap(terms), 0, 1).reshape(8, MID, QUARTER)
    summed = jnp.zeros((MID, QUARTER), F32)
    for o in offsets:
        slot = o - start
        out = lax.dynamic_index_in_dim(slots, jnp.clip(slot, 0, 7), 0, keepdims=False)
        out = jnp.where((slot >= 0) & (slot < 8), out, jnp.zeros_like(out))
        summed = summed + (out if o == 0 else shifted(out, "rows", o)).astype(F32)
    high, low = halves(summed)
    wide = dot(proj_weight, high, 0, 0) + dot(proj_weight, low, 0, 0)
    target_share = jnp.swapaxes(swap(wide.reshape(BANDS, SHARE, QUARTER)), 1, 2)
    source_share = jnp.sum(swap(share).astype(F32), axis=0).T
    shape_out = (ROWS_DEV, PIXELS // ROWS_DEV, SHARE)
    return pyramid, source_share.reshape(shape_out), target_share.reshape(shape_out)


def solution(mesh):
    in_specs = (
        P(None, "rows", None, None),
        P(),
        P(),
        P("rows"),
        P("rows"),
        P("rows", None, "band", None, None),
    )
    out_specs = (
        P("rows", None, "band", None, None),
        P("rows", None, "band"),
        P("rows", None, "band"),
    )
    return jax.shard_map(shards, mesh=mesh, in_specs=in_specs, out_specs=out_specs, check_vma=False)
```

time: 288 us -> 149 us (0.52)
  the two profiles are of different devices: /device:TPU:1 before, /device:TPU:256 now
where the time goes in v1:
time: 149 us; the launch traced here: 148 us
  starting transfers between devices  97.3 us (65%)
  waiting for transfers between devices  21.9 us (15%)
  local copies, waits for them, and re-layouts  16.4 us (11%)
  Pallas kernels  6.57 us (4%)
  matrix products  2.99 us (2%)
  between operations  2.84 us (2%)
    ppermute x17, starting transfers between devices, shifted(): return lax.ppermute(x, axis, pairs)  55.8 us
    ppermute x12, starting transfers between devices, swap(): lax.ppermute(out, 'band', [(i, (i + d) % BANDS) for i in range(BANDS)])  41.5 us
    ppermute x17, waiting for transfers between devices, shifted(): return lax.ppermute(x, axis, pairs)  17.8 us
    unnamed x22, local copies, waits for them, and re-layouts  8.98 us
    pallas_call x1, Pallas kernels, tiles(): pl.pallas_call(tile_kernel, grid=(2,), in_specs=[pl.BlockSpec(memory_spac...  6.57 us
    ppermute x12, waiting for transfers between devices, swap(): lax.ppermute(out, 'band', [(i, (i + d) % BANDS) for i in range(BANDS)])  4.1 us
  transfers between devices with their start and end apart: 29, of which 6 were waited for; matrix products, arithmetic and copies ran while one was open for 6% of the time, Pallas kernels for 0%

profile of v1, /device:TPU:256, one launch (start us, length us, event | category | flops | bytes accessed | tf_op | source)
XLA Modules:
  0.0 148.3 jit_solution(18269481595315229635)
XLA Ops:
  0.6 2.5 %copy.13 = bf16[2,4,512,96]{3,0,2,1:T(2,128)(2,1)S(1)} copy(bf16[2,4,512,96]{2,3,1,0:T(8,128)(2,1)} %param.6) | data formatting | bytes 1572864 | tf_op args[0]
  6.0 8.3 %collective-permute-done = bf16[2,1,512,96]{3,0,2,1:T(2,128)(2,1)S(1)} collective-permute-done((bf16[2,1,512,96]{3,0,2,1:T(2,128)(2,1)S(1)}, bf16[2,1,512,96]{3,0,2,1:T(2,128)(2,1)S(1)}, u32[]{:S(2)}, u32[]{:S(2)}) %collective-permute-start) | collective-permute-done | bytes 196640 | tf_op jit(solution)/shard_map/ppermute | solution.py:24
  14.3 2.6 %fusion.2 = bf16[2,2,256,128]{3,0,2,1:T(2,128)(2,1)S(1)} fusion(bf16[3,3,96,128]{3,2,1,0:T(8,128)(2,1)S(1)} %copy-done, bf16[2,4,512,96]{3,0,2,1:T(2,128)(2,1)S(1)} %copy.13, bf16[2,1,512,96]{3,0,2,1:T(2,128)(2,1)S(1)} %collective-permute-done), kind=kOutput, calls=%fused_computation.8 | convolution fusion | flops 228425728 | bytes 1466368 | tf_op jit(solution)/shard_map/conv_general_dilated | solution.py:124
  19.4 2.5 %copy.16.grad_ref = bf16[1,2,1,512,960]{4,3,2,1,0:T(8,128)(2,1)} copy(bf16[1,2,1,512,960]{3,4,2,1,0:T(8,128)(2,1)S(1)} %copy-done.2) | data formatting | bytes 3932160 | tf_op args[5]
  22.7 2.5 %collective-permute-start.2 = (bf16[128,128]{1,0:T(8,128)(2,1)S(1)}, bf16[128,128]{1,0:T(8,128)(2,1)S(1)}, u32[]{:S(2)}, u32[]{:S(2)}) collective-permute-start(bf16[128,128]{1,0:T(8,128)(2,1)S(1)} %constant_dynamic-slice_fusion.4), channel_id=1, source_target_pairs={{0,12},{4,16},{8,20},{12,24},{16,28},{20,32},{24,36},{28,40},{32,4... | collective-permute-start | bytes 98312 | tf_op jit(solution)/shard_map/ppermute | solution.py:24
  25.2 2.6 %collective-permute-start.3 = (bf16[128,128]{1,0:T(8,128)(2,1)S(1)}, bf16[128,128]{1,0:T(8,128)(2,1)S(1)}, u32[]{:S(2)}, u32[]{:S(2)}) collective-permute-start(bf16[128,128]{1,0:T(8,128)(2,1)S(1)} %constant_dynamic-slice_fusion.4), channel_id=1, source_target_pairs={{0,8},{4,12},{8,16},{12,20},{16,24},{20,28},{24,32},{28,36},{32,40... | collective-permute-start | bytes 98312 | tf_op jit(solution)/shard_map/ppermute | solution.py:24
  27.8 5.0 %collective-permute-start.4 = (bf16[128,128]{1,0:T(8,128)(2,1)S(1)}, bf16[128,128]{1,0:T(8,128)(2,1)S(1)}, u32[]{:S(2)}, u32[]{:S(2)}) collective-permute-start(bf16[128,128]{1,0:T(8,128)(2,1)S(1)} %constant_dynamic-slice_fusion.4), channel_id=1, source_target_pairs={{0,4},{4,8},{8,12},{12,16},{16,20},{20,24},{24,28},{28,32},{32,36}... | collective-permute-start | bytes 98312 | tf_op jit(solution)/shard_map/ppermute | solution.py:24
  32.8 6.6 %collective-permute-start.5 = (bf16[128,128]{1,0:T(8,128)(2,1)S(1)}, bf16[128,128]{1,0:T(8,128)(2,1)S(1)}, u32[]{:S(2)}, u32[]{:S(2)}) collective-permute-start(bf16[128,128]{1,0:T(8,128)(2,1)S(1)} %constant_dynamic-slice_fusion.4), channel_id=1, source_target_pairs={{4,0},{8,4},{12,8},{16,12},{20,16},{24,20},{28,24},{32,28},{36,32}... | collective-permute-start | bytes 98312 | tf_op jit(solution)/shard_map/ppermute | solution.py:24
  43.7 4.5 %collective-permute-start.8 = (bf16[128,128]{1,0:T(8,128)(2,1)S(1)}, bf16[128,128]{1,0:T(8,128)(2,1)S(1)}, u32[]{:S(2)}, u32[]{:S(2)}) collective-permute-start(bf16[128,128]{1,0:T(8,128)(2,1)S(1)} %constant_dynamic-slice_fusion.4), channel_id=1, source_target_pairs={{16,0},{20,4},{24,8},{28,12},{32,16},{36,20},{40,24},{44,28},{48,3... | collective-permute-start | bytes 98312 | tf_op jit(solution)/shard_map/ppermute | solution.py:24
  51.1 3.4 %collective-permute-start.9 = (bf16[2,128,128]{2,1,0:T(8,128)(2,1)S(1)}, bf16[2,128,128]{2,1,0:T(8,128)(2,1)S(1)}, u32[]{:S(2)}, u32[]{:S(2)}) collective-permute-start(bf16[2,128,128]{2,1,0:T(8,128)(2,1)S(1)} %get-tuple-element.33), channel_id=1, source_target_pairs={{0,1},{1,2},{2,3},{3,0},{4,5},{5,6},{6,7},{7,4},{8,9},{9,10},{10,1... | collective-permute-start | bytes 196616 | tf_op jit(solution)/shard_map/ppermute | solution.py:116
  54.5 4.6 %collective-permute-start.10 = (bf16[2,128,128]{2,1,0:T(8,128)(2,1)S(1)}, bf16[2,128,128]{2,1,0:T(8,128)(2,1)S(1)}, u32[]{:S(2)}, u32[]{:S(2)}) collective-permute-start(bf16[2,128,128]{2,1,0:T(8,128)(2,1)S(1)} %get-tuple-element.32), channel_id=1, source_target_pairs={{0,2},{1,3},{2,0},{3,1},{4,6},{5,7},{6,4},{7,5},{8,10},{9,11},{10,... | collective-permute-start | bytes 196616 | tf_op jit(solution)/shard_map/ppermute | solution.py:116
  59.1 3.3 %collective-permute-start.11 = (bf16[2,128,128]{2,1,0:T(8,128)(2,1)S(1)}, bf16[2,128,128]{2,1,0:T(8,128)(2,1)S(1)}, u32[]{:S(2)}, u32[]{:S(2)}) collective-permute-start(bf16[2,128,128]{2,1,0:T(8,128)(2,1)S(1)} %get-tuple-element.34), channel_id=1, source_target_pairs={{0,3},{1,0},{2,1},{3,2},{4,7},{5,4},{6,5},{7,6},{8,11},{9,8},{10,9... | collective-permute-start | bytes 196616 | tf_op jit(solution)/shard_map/ppermute | solution.py:116
  66.7 6.6 %shard_map.85 = (bf16[1,2,1,512,960]{4,3,2,1,0:T(8,128)(2,1)}, bf16[4,2,128,128]{3,2,1,0:T(8,128)(2,1)}, bf16[4,64,512]{2,1,0:T(8,128)(2,1)}) custom-call(s32[1]{0:T(128)S(6)} %copy.37.count_ref, bf16[512,128]{1,0:T(8,128)(2,1)} %bitcast.123, bf16[2,512,128]{2,1,0:T(8,128)(2,1)} %bitcast.122, bf16[1,2,1,512,960]{4,3,2,1,0:T(8,128)(2,1)} %copy.16.grad_ref, ...), custom_call_target="tpu_custom_call" | custom-call | tf_op jit(solution)/shard_map/pallas_call | solution.py:83
  76.3 6.0 %collective-permute-start.16 = (bf16[2,128,128]{2,1,0:T(8,128)(2,1)S(1)}, bf16[2,128,128]{2,1,0:T(8,128)(2,1)S(1)}, u32[]{:S(2)}, u32[]{:S(2)}) collective-permute-start(bf16[2,128,128]{2,1,0:T(8,128)(2,1)S(1)} %get-tuple-element.25), channel_id=1, source_target_pairs={{0,2},{1,3},{2,0},{3,1},{4,6},{5,7},{6,4},{7,5},{8,10},{9,11},{10,... | collective-permute-start | bytes 196616 | tf_op jit(solution)/shard_map/ppermute | solution.py:116
  85.2 3.9 %collective-permute-start.12 = (bf16[64,512]{1,0:T(8,128)(2,1)S(1)}, bf16[64,512]{1,0:T(8,128)(2,1)S(1)}, u32[]{:S(2)}, u32[]{:S(2)}) collective-permute-start(bf16[64,512]{1,0:T(8,128)(2,1)S(1)} %get-tuple-element.30), channel_id=1, source_target_pairs={{0,1},{1,2},{2,3},{3,0},{4,5},{5,6},{6,7},{7,4},{8,9},{9,10},{10,1... | collective-permute-start | bytes 196616 | tf_op jit(solution)/shard_map/ppermute | solution.py:116
  91.1 4.5 %collective-permute-start.14 = (bf16[64,512]{1,0:T(8,128)(2,1)S(1)}, bf16[64,512]{1,0:T(8,128)(2,1)S(1)}, u32[]{:S(2)}, u32[]{:S(2)}) collective-permute-start(bf16[64,512]{1,0:T(8,128)(2,1)S(1)} %get-tuple-element.28), channel_id=1, source_target_pairs={{0,3},{1,0},{2,1},{3,2},{4,7},{5,4},{6,5},{7,6},{8,11},{9,8},{10,9... | collective-permute-start | bytes 196616 | tf_op jit(solution)/shard_map/ppermute | solution.py:116
  96.4 7.8 %collective-permute-start.18 = (bf16[128,128]{1,0:T(8,128)(2,1)S(1)}, bf16[128,128]{1,0:T(8,128)(2,1)S(1)}, u32[]{:S(2)}, u32[]{:S(2)}) collective-permute-start(bf16[128,128]{1,0:T(8,128)(2,1)S(1)} %get-tuple-element.15), channel_id=1, source_target_pairs={{16,0},{20,4},{24,8},{28,12},{32,16},{36,20},{40,24},{44,28},{48,3... | collective-permute-start | bytes 98312 | tf_op jit(solution)/shard_map/ppermute | solution.py:24
  108.1 2.5 %copy.20 = bf16[1,2,1,512,960]{3,4,2,1,0:T(8,128)(2,1)} copy(bf16[1,2,1,512,960]{4,3,2,1,0:T(8,128)(2,1)S(1)} %copy-done.1) | data formatting | bytes 3932160
  115.0 3.9 %collective-permute-start.23 = (bf16[128,128]{1,0:T(8,128)(2,1)S(1)}, bf16[128,128]{1,0:T(8,128)(2,1)S(1)}, u32[]{:S(2)}, u32[]{:S(2)}) collective-permute-start(bf16[128,128]{1,0:T(8,128)(2,1)S(1)} %get-tuple-element.18), channel_id=1, source_target_pairs={{0,8},{4,12},{8,16},{12,20},{16,24},{20,28},{24,32},{28,36},{32,40... | collective-permute-start | bytes 98312 | tf_op jit(solution)/shard_map/ppermute | solution.py:24
  118.9 4.3 %collective-permute-start.24 = (bf16[128,128]{1,0:T(8,128)(2,1)S(1)}, bf16[128,128]{1,0:T(8,128)(2,1)S(1)}, u32[]{:S(2)}, u32[]{:S(2)}) collective-permute-start(bf16[128,128]{1,0:T(8,128)(2,1)S(1)} %get-tuple-element.17), channel_id=1, source_target_pairs={{0,12},{4,16},{8,20},{12,24},{16,28},{20,32},{24,36},{28,40},{32,4... | collective-permute-start | bytes 98312 | tf_op jit(solution)/shard_map/ppermute | solution.py:24
  126.3 2.4 %collective-permute-done.24 = bf16[128,128]{1,0:T(8,128)(2,1)S(1)} collective-permute-done((bf16[128,128]{1,0:T(8,128)(2,1)S(1)}, bf16[128,128]{1,0:T(8,128)(2,1)S(1)}, u32[]{:S(2)}, u32[]{:S(2)}) %collective-permute-start.24) | collective-permute-done | bytes 32800 | tf_op jit(solution)/shard_map/ppermute | solution.py:24
  128.7 5.0 %collective-permute-done.25 = bf16[128,128]{1,0:T(8,128)(2,1)S(1)} collective-permute-done((bf16[128,128]{1,0:T(8,128)(2,1)S(1)}, bf16[128,128]{1,0:T(8,128)(2,1)S(1)}, u32[]{:S(2)}, u32[]{:S(2)}) %collective-permute-start.25) | collective-permute-done | bytes 32800 | tf_op jit(solution)/shard_map/ppermute | solution.py:24
  136.2 4.8 %collective-permute-start.27 = (f32[64,128]{1,0:T(8,128)S(1)}, f32[64,128]{1,0:T(8,128)S(1)}, u32[]{:S(2)}, u32[]{:S(2)}) collective-permute-start(f32[64,128]{1,0:T(8,128)S(1)} %get-tuple-element.39), channel_id=1, source_target_pairs={{0,2},{1,3},{2,0},{3,1},{4,6},{5,7},{6,4},{7,5},{8,10},{9,11},{10,... | collective-permute-start | bytes 98312 | tf_op jit(solution)/shard_map/ppermute | solution.py:116
  141.0 3.1 %collective-permute-start.28 = (f32[64,128]{1,0:T(8,128)S(1)}, f32[64,128]{1,0:T(8,128)S(1)}, u32[]{:S(2)}, u32[]{:S(2)}) collective-permute-start(f32[64,128]{1,0:T(8,128)S(1)} %get-tuple-element.38), channel_id=1, source_target_pairs={{0,3},{1,0},{2,1},{3,2},{4,7},{5,4},{6,5},{7,6},{8,11},{9,8},{10,9... | collective-permute-start | bytes 98312 | tf_op jit(solution)/shard_map/ppermute | solution.py:116
  (92 shorter events, 42.0 us)
Async XLA Ops:
  3.3 11.0 %collective-permute-start = (bf16[2,1,512,96]{3,0,2,1:T(2,128)(2,1)S(1)}, bf16[2,1,512,96]{3,0,2,1:T(2,128)(2,1)S(1)}, u32[]{:S(2)}, u32[]{:S(2)}) collective-permute-start(bf16[2,1,512,96]{3,0,2,1:T(2,128)(2,1)S(1)} %slice.24), channel_id=1, source_target_pairs={{0,4},{4,8},{8,12},{12,16},{16,20},{20,24},{24,28},{28,32},{32,36}... | collective-permute-start | bytes 589832 | tf_op jit(solution)/shard_map/ppermute | solution.py:24
  17.3 22.1 %collective-permute-start.1 = (bf16[128,128]{1,0:T(8,128)(2,1)S(1)}, bf16[128,128]{1,0:T(8,128)(2,1)S(1)}, u32[]{:S(2)}, u32[]{:S(2)}) collective-permute-start(bf16[128,128]{1,0:T(8,128)(2,1)S(1)} %constant_dynamic-slice_fusion.4), channel_id=1, source_target_pairs={{0,16},{4,20},{8,24},{12,28},{16,32},{20,36},{24,40},{28,44},{32,4... | collective-permute-start | bytes 98312 | tf_op jit(solution)/shard_map/ppermute | solution.py:24
  22.7 19.1 %collective-permute-start.2 = (bf16[128,128]{1,0:T(8,128)(2,1)S(1)}, bf16[128,128]{1,0:T(8,128)(2,1)S(1)}, u32[]{:S(2)}, u32[]{:S(2)}) collective-permute-start(bf16[128,128]{1,0:T(8,128)(2,1)S(1)} %constant_dynamic-slice_fusion.4), channel_id=1, source_target_pairs={{0,12},{4,16},{8,20},{12,24},{16,28},{20,32},{24,36},{28,40},{32,4... | collective-permute-start | bytes 98312 | tf_op jit(solution)/shard_map/ppermute | solution.py:24
  25.2 18.5 %collective-permute-start.3 = (bf16[128,128]{1,0:T(8,128)(2,1)S(1)}, bf16[128,128]{1,0:T(8,128)(2,1)S(1)}, u32[]{:S(2)}, u32[]{:S(2)}) collective-permute-start(bf16[128,128]{1,0:T(8,128)(2,1)S(1)} %constant_dynamic-slice_fusion.4), channel_id=1, source_target_pairs={{0,8},{4,12},{8,16},{12,20},{16,24},{20,28},{24,32},{28,36},{32,40... | collective-permute-start | bytes 98312 | tf_op jit(solution)/shard_map/ppermute | solution.py:24
  27.8 20.5 %collective-permute-start.4 = (bf16[128,128]{1,0:T(8,128)(2,1)S(1)}, bf16[128,128]{1,0:T(8,128)(2,1)S(1)}, u32[]{:S(2)}, u32[]{:S(2)}) collective-permute-start(bf16[128,128]{1,0:T(8,128)(2,1)S(1)} %constant_dynamic-slice_fusion.4), channel_id=1, source_target_pairs={{0,4},{4,8},{8,12},{12,16},{16,20},{20,24},{24,28},{28,32},{32,36}... | collective-permute-start | bytes 98312 | tf_op jit(solution)/shard_map/ppermute | solution.py:24
  32.8 15.5 %collective-permute-start.5 = (bf16[128,128]{1,0:T(8,128)(2,1)S(1)}, bf16[128,128]{1,0:T(8,128)(2,1)S(1)}, u32[]{:S(2)}, u32[]{:S(2)}) collective-permute-start(bf16[128,128]{1,0:T(8,128)(2,1)S(1)} %constant_dynamic-slice_fusion.4), channel_id=1, source_target_pairs={{4,0},{8,4},{12,8},{16,12},{20,16},{24,20},{28,24},{32,28},{36,32}... | collective-permute-start | bytes 98312 | tf_op jit(solution)/shard_map/ppermute | solution.py:24
  39.4 8.9 %collective-permute-start.6 = (bf16[128,128]{1,0:T(8,128)(2,1)S(1)}, bf16[128,128]{1,0:T(8,128)(2,1)S(1)}, u32[]{:S(2)}, u32[]{:S(2)}) collective-permute-start(bf16[128,128]{1,0:T(8,128)(2,1)S(1)} %constant_dynamic-slice_fusion.4), channel_id=1, source_target_pairs={{8,0},{12,4},{16,8},{20,12},{24,16},{28,20},{32,24},{36,28},{40,32... | collective-permute-start | bytes 98312 | tf_op jit(solution)/shard_map/ppermute | solution.py:24
  51.1 12.1 %collective-permute-start.9 = (bf16[2,128,128]{2,1,0:T(8,128)(2,1)S(1)}, bf16[2,128,128]{2,1,0:T(8,128)(2,1)S(1)}, u32[]{:S(2)}, u32[]{:S(2)}) collective-permute-start(bf16[2,128,128]{2,1,0:T(8,128)(2,1)S(1)} %get-tuple-element.33), channel_id=1, source_target_pairs={{0,1},{1,2},{2,3},{3,0},{4,5},{5,6},{6,7},{7,4},{8,9},{9,10},{10,1... | collective-permute-start | bytes 196616 | tf_op jit(solution)/shard_map/ppermute | solution.py:116
  54.5 8.7 %collective-permute-start.10 = (bf16[2,128,128]{2,1,0:T(8,128)(2,1)S(1)}, bf16[2,128,128]{2,1,0:T(8,128)(2,1)S(1)}, u32[]{:S(2)}, u32[]{:S(2)}) collective-permute-start(bf16[2,128,128]{2,1,0:T(8,128)(2,1)S(1)} %get-tuple-element.32), channel_id=1, source_target_pairs={{0,2},{1,3},{2,0},{3,1},{4,6},{5,7},{6,4},{7,5},{8,10},{9,11},{10,... | collective-permute-start | bytes 196616 | tf_op jit(solution)/shard_map/ppermute | solution.py:116
  74.4 16.7 %collective-permute-start.15 = (bf16[2,128,128]{2,1,0:T(8,128)(2,1)S(1)}, bf16[2,128,128]{2,1,0:T(8,128)(2,1)S(1)}, u32[]{:S(2)}, u32[]{:S(2)}) collective-permute-start(bf16[2,128,128]{2,1,0:T(8,128)(2,1)S(1)} %get-tuple-element.26), channel_id=1, source_target_pairs={{0,1},{1,2},{2,3},{3,0},{4,5},{5,6},{6,7},{7,4},{8,9},{9,10},{10,1... | collective-permute-start | bytes 196616 | tf_op jit(solution)/shard_map/ppermute | solution.py:116
  76.3 19.4 %collective-permute-start.16 = (bf16[2,128,128]{2,1,0:T(8,128)(2,1)S(1)}, bf16[2,128,128]{2,1,0:T(8,128)(2,1)S(1)}, u32[]{:S(2)}, u32[]{:S(2)}) collective-permute-start(bf16[2,128,128]{2,1,0:T(8,128)(2,1)S(1)} %get-tuple-element.25), channel_id=1, source_target_pairs={{0,2},{1,3},{2,0},{3,1},{4,6},{5,7},{6,4},{7,5},{8,10},{9,11},{10,... | collective-permute-start | bytes 196616 | tf_op jit(solution)/shard_map/ppermute | solution.py:116
  82.3 13.4 %collective-permute-start.17 = (bf16[2,128,128]{2,1,0:T(8,128)(2,1)S(1)}, bf16[2,128,128]{2,1,0:T(8,128)(2,1)S(1)}, u32[]{:S(2)}, u32[]{:S(2)}) collective-permute-start(bf16[2,128,128]{2,1,0:T(8,128)(2,1)S(1)} %get-tuple-element.24), channel_id=1, source_target_pairs={{0,3},{1,0},{2,1},{3,2},{4,7},{5,4},{6,5},{7,6},{8,11},{9,8},{10,9... | collective-permute-start | bytes 196616 | tf_op jit(solution)/shard_map/ppermute | solution.py:116
  85.2 21.0 %collective-permute-start.12 = (bf16[64,512]{1,0:T(8,128)(2,1)S(1)}, bf16[64,512]{1,0:T(8,128)(2,1)S(1)}, u32[]{:S(2)}, u32[]{:S(2)}) collective-permute-start(bf16[64,512]{1,0:T(8,128)(2,1)S(1)} %get-tuple-element.30), channel_id=1, source_target_pairs={{0,1},{1,2},{2,3},{3,0},{4,5},{5,6},{6,7},{7,4},{8,9},{9,10},{10,1... | collective-permute-start | bytes 196616 | tf_op jit(solution)/shard_map/ppermute | solution.py:116
  89.1 21.5 %collective-permute-start.13 = (bf16[64,512]{1,0:T(8,128)(2,1)S(1)}, bf16[64,512]{1,0:T(8,128)(2,1)S(1)}, u32[]{:S(2)}, u32[]{:S(2)}) collective-permute-start(bf16[64,512]{1,0:T(8,128)(2,1)S(1)} %get-tuple-element.29), channel_id=1, source_target_pairs={{0,2},{1,3},{2,0},{3,1},{4,6},{5,7},{6,4},{7,5},{8,10},{9,11},{10,... | collective-permute-start | bytes 196616 | tf_op jit(solution)/shard_map/ppermute | solution.py:116
  91.1 21.8 %collective-permute-start.14 = (bf16[64,512]{1,0:T(8,128)(2,1)S(1)}, bf16[64,512]{1,0:T(8,128)(2,1)S(1)}, u32[]{:S(2)}, u32[]{:S(2)}) collective-permute-start(bf16[64,512]{1,0:T(8,128)(2,1)S(1)} %get-tuple-element.28), channel_id=1, source_target_pairs={{0,3},{1,0},{2,1},{3,2},{4,7},{5,4},{6,5},{7,6},{8,11},{9,8},{10,9... | collective-permute-start | bytes 196616 | tf_op jit(solution)/shard_map/ppermute | solution.py:116
  96.4 18.6 %collective-permute-start.18 = (bf16[128,128]{1,0:T(8,128)(2,1)S(1)}, bf16[128,128]{1,0:T(8,128)(2,1)S(1)}, u32[]{:S(2)}, u32[]{:S(2)}) collective-permute-start(bf16[128,128]{1,0:T(8,128)(2,1)S(1)} %get-tuple-element.15), channel_id=1, source_target_pairs={{16,0},{20,4},{24,8},{28,12},{32,16},{36,20},{40,24},{44,28},{48,3... | collective-permute-start | bytes 98312 | tf_op jit(solution)/shard_map/ppermute | solution.py:24
  104.2 14.7 %collective-permute-start.19 = (bf16[128,128]{1,0:T(8,128)(2,1)S(1)}, bf16[128,128]{1,0:T(8,128)(2,1)S(1)}, u32[]{:S(2)}, u32[]{:S(2)}) collective-permute-start(bf16[128,128]{1,0:T(8,128)(2,1)S(1)} %get-tuple-element.22), channel_id=1, source_target_pairs={{12,0},{16,4},{20,8},{24,12},{28,16},{32,20},{36,24},{40,28},{44,3... | collective-permute-start | bytes 98312 | tf_op jit(solution)/shard_map/ppermute | solution.py:24
  106.2 17.1 %collective-permute-start.20 = (bf16[128,128]{1,0:T(8,128)(2,1)S(1)}, bf16[128,128]{1,0:T(8,128)(2,1)S(1)}, u32[]{:S(2)}, u32[]{:S(2)}) collective-permute-start(bf16[128,128]{1,0:T(8,128)(2,1)S(1)} %get-tuple-element.21), channel_id=1, source_target_pairs={{8,0},{12,4},{16,8},{20,12},{24,16},{28,20},{32,24},{36,28},{40,32... | collective-permute-start | bytes 98312 | tf_op jit(solution)/shard_map/ppermute | solution.py:24
  110.7 15.6 %collective-permute-start.21 = (bf16[128,128]{1,0:T(8,128)(2,1)S(1)}, bf16[128,128]{1,0:T(8,128)(2,1)S(1)}, u32[]{:S(2)}, u32[]{:S(2)}) collective-permute-start(bf16[128,128]{1,0:T(8,128)(2,1)S(1)} %get-tuple-element.20), channel_id=1, source_target_pairs={{4,0},{8,4},{12,8},{16,12},{20,16},{24,20},{28,24},{32,28},{36,32}... | collective-permute-start | bytes 98312 | tf_op jit(solution)/shard_map/ppermute | solution.py:24
  112.9 13.4 %collective-permute-start.22 = (bf16[128,128]{1,0:T(8,128)(2,1)S(1)}, bf16[128,128]{1,0:T(8,128)(2,1)S(1)}, u32[]{:S(2)}, u32[]{:S(2)}) collective-permute-start(bf16[128,128]{1,0:T(8,128)(2,1)S(1)} %get-tuple-element.19), channel_id=1, source_target_pairs={{0,4},{4,8},{8,12},{12,16},{16,20},{20,24},{24,28},{28,32},{32,36}... | collective-permute-start | bytes 98312 | tf_op jit(solution)/shard_map/ppermute | solution.py:24
  115.0 11.2 %collective-permute-start.23 = (bf16[128,128]{1,0:T(8,128)(2,1)S(1)}, bf16[128,128]{1,0:T(8,128)(2,1)S(1)}, u32[]{:S(2)}, u32[]{:S(2)}) collective-permute-start(bf16[128,128]{1,0:T(8,128)(2,1)S(1)} %get-tuple-element.18), channel_id=1, source_target_pairs={{0,8},{4,12},{8,16},{12,20},{16,24},{20,28},{24,32},{28,36},{32,40... | collective-permute-start | bytes 98312 | tf_op jit(solution)/shard_map/ppermute | solution.py:24
  118.9 9.7 %collective-permute-start.24 = (bf16[128,128]{1,0:T(8,128)(2,1)S(1)}, bf16[128,128]{1,0:T(8,128)(2,1)S(1)}, u32[]{:S(2)}, u32[]{:S(2)}) collective-permute-start(bf16[128,128]{1,0:T(8,128)(2,1)S(1)} %get-tuple-element.17), channel_id=1, source_target_pairs={{0,12},{4,16},{8,20},{12,24},{16,28},{20,32},{24,36},{28,40},{32,4... | collective-permute-start | bytes 98312 | tf_op jit(solution)/shard_map/ppermute | solution.py:24
  123.3 10.4 %collective-permute-start.25 = (bf16[128,128]{1,0:T(8,128)(2,1)S(1)}, bf16[128,128]{1,0:T(8,128)(2,1)S(1)}, u32[]{:S(2)}, u32[]{:S(2)}) collective-permute-start(bf16[128,128]{1,0:T(8,128)(2,1)S(1)} %get-tuple-element.16), channel_id=1, source_target_pairs={{0,16},{4,20},{8,24},{12,28},{16,32},{20,36},{24,40},{28,44},{32,4... | collective-permute-start | bytes 98312 | tf_op jit(solution)/shard_map/ppermute | solution.py:24
  134.3 10.6 %collective-permute-start.26 = (f32[64,128]{1,0:T(8,128)S(1)}, f32[64,128]{1,0:T(8,128)S(1)}, u32[]{:S(2)}, u32[]{:S(2)}) collective-permute-start(f32[64,128]{1,0:T(8,128)S(1)} %get-tuple-element.40), channel_id=1, source_target_pairs={{0,1},{1,2},{2,3},{3,0},{4,5},{5,6},{6,7},{7,4},{8,9},{9,10},{10,1... | collective-permute-start | bytes 98312 | tf_op jit(solution)/shard_map/ppermute | solution.py:116
  (9 other events, 113.2 us)

commit v2 on v1

v2 whole, which is shorter than its diff:
```python
import jax
import jax.numpy as jnp
from jax import lax
from jax.experimental import pallas as pl
from jax.experimental.pallas import tpu as pltpu
from jax.sharding import PartitionSpec as P

ROWS_DEV = 2
BAND_REACH = 4
PIXELS = 512
MID = 128
LOWER = 448
BANDS = 4
QUARTER = PIXELS // BANDS
SHARE = 64
SCALE = 1.0 / 16.0
F32 = jnp.float32
BF16 = jnp.bfloat16
MESH = pl.DeviceIdType.MESH
OFFSETS = (-4, 4, -3, 3, -2, 2, -1, 1)


def shifted(x, axis, by):
    size = lax.axis_size(axis)
    pairs = [(i, i + by) for i in range(size) if 0 <= i + by < size]
    return lax.ppermute(x, axis, pairs)


def halves(x):
    high = x.astype(BF16)
    return high, (x - high.astype(F32)).astype(BF16)


def dot(a, b, da=1, db=0):
    return lax.dot_general(a, b, (((da,), (db,)), ((), ())), preferred_element_type=F32)


def tile_kernel(count_ref, source_ref, target_ref, grad_ref, proj_ref, pyramid_ref, terms_ref, share_ref, pool, spread, pair, total):
    j = pl.program_id(0)
    source = source_ref[...]

    @pl.when(j == 0)
    def _():
        row = lax.broadcasted_iota(jnp.int32, (LOWER, PIXELS), 0)
        column = lax.broadcasted_iota(jnp.int32, (LOWER, PIXELS), 1)
        shift = jnp.where(row < 256, 1, jnp.where(row < 384, 2, 3))
        first = jnp.where(row < 256, 0, jnp.where(row < 384, 256, 384))
        weight = jnp.where(row < 256, 0.5, jnp.where(row < 384, 0.25, 0.125))
        pool[...] = jnp.where((column >> shift) == row - first, weight, 0.0).astype(BF16)
        square_high, square_low = halves(dot(proj_ref[...], proj_ref[...], 1, 1) * SCALE)
        high, low = halves(dot(source, square_high) + dot(source, square_low))
        pair[...] = jnp.concatenate([high, low], axis=1)
        row = lax.broadcasted_iota(jnp.int32, (PIXELS, LOWER), 0)
        column = lax.broadcasted_iota(jnp.int32, (PIXELS, LOWER), 1)
        shift = jnp.where(column < 256, 1, jnp.where(column < 384, 2, 3))
        first = jnp.where(column < 256, 0, jnp.where(column < 384, 256, 384))
        weight = jnp.where(column < 256, 0.5, jnp.where(column < 384, 0.25, 0.125))
        spread[...] = jnp.where((row >> shift) == column - first, weight, 0.0).astype(BF16)

    valid = j * BANDS + lax.axis_index("band") < count_ref[0]
    target = target_ref[0]
    grad = grad_ref[0, 0, 0]
    high, low = halves(dot(pool[...], target))
    base = dot(jnp.concatenate([target, target], axis=1), pair[...], 1, 1)
    rest = dot(jnp.concatenate([high, high], axis=1), pair[...], 1, 1) + dot(low, pair[:, :MID], 1, 1)
    pyramid_ref[0, 0, 0, :PIXELS] = jnp.where(valid, base, 0.0).astype(BF16)
    pyramid_ref[0, 0, 0, PIXELS:] = jnp.where(valid, rest, 0.0).astype(BF16)
    both = dot(jnp.concatenate([high, low], axis=1), grad[PIXELS:], 0, 0)
    part = jnp.where(valid, dot(target, grad[:PIXELS], 0, 0) + both[:MID] + both[MID:], 0.0)
    gathered = dot(grad, source)
    both = dot(spread[...], jnp.concatenate(halves(gathered[PIXELS:]), axis=1))
    term = (gathered[:PIXELS] + both[:, :MID] + both[:, MID:]) * SCALE
    term = jnp.where(valid, term, 0.0).astype(BF16)
    for q in range(BANDS):
        terms_ref[q, 0] = term[q * QUARTER : (q + 1) * QUARTER]

    @pl.when(j == 0)
    def _():
        total[...] = part

    @pl.when(j == 1)
    def _():
        high, low = halves((total[...] + part) * SCALE)
        proj = proj_ref[...]
        wide = dot(proj, high, 0, 0) + dot(proj, low, 0, 0)
        for q in range(BANDS):
            share_ref[q] = wide[q * SHARE : (q + 1) * SHARE].astype(BF16)


def tiles(count, source, target, grad, proj):
    return pl.pallas_call(
        tile_kernel,
        grid=(2,),
        in_specs=[
            pl.BlockSpec(memory_space=pltpu.SMEM),
            pl.BlockSpec((PIXELS, MID), lambda j: (0, 0)),
            pl.BlockSpec((1, PIXELS, MID), lambda j: (j, 0, 0)),
            pl.BlockSpec((1, 1, 1, 960, PIXELS), lambda j: (0, j, 0, 0, 0)),
            pl.BlockSpec((MID, 256), lambda j: (0, 0)),
        ],
        out_specs=[
            pl.BlockSpec((1, 1, 1, 960, PIXELS), lambda j: (0, j, 0, 0, 0)),
            pl.BlockSpec((BANDS, 1, QUARTER, MID), lambda j: (0, j, 0, 0)),
            pl.BlockSpec((BANDS, SHARE, PIXELS), lambda j: (0, 0, 0)),
        ],
        out_shape=[
            jax.ShapeDtypeStruct((1, 2, 1, 960, PIXELS), BF16),
            jax.ShapeDtypeStruct((BANDS, 2, QUARTER, MID), BF16),
            jax.ShapeDtypeStruct((BANDS, SHARE, PIXELS), BF16),
        ],
        scratch_shapes=[
            pltpu.VMEM((LOWER, PIXELS), BF16),
            pltpu.VMEM((PIXELS, LOWER), BF16),
            pltpu.VMEM((PIXELS, 2 * MID), BF16),
            pltpu.VMEM((MID, PIXELS), F32),
        ],
    )(count, source, target, grad, proj)


def band_peers():
    here = lax.axis_index("band")
    return here, [lax.rem(here + d, BANDS) for d in range(BANDS)]


def row_peer(offset):
    size = lax.axis_size("rows")
    return lax.rem(lax.axis_index("rows") + offset + size, size)


def in_frame(offset):
    block = lax.axis_index("rows") + offset
    return (block >= 0) & (block < lax.axis_size("rows"))


def meet(peers):
    barrier = pltpu.get_barrier_semaphore()
    for o in OFFSETS:
        pl.semaphore_signal(barrier, inc=1, device_id={"rows": row_peer(o)}, device_id_type=MESH)
    for d in range(1, BANDS):
        pl.semaphore_signal(barrier, inc=1, device_id={"band": peers[d]}, device_id_type=MESH)
    pl.semaphore_wait(barrier, len(OFFSETS) + BANDS - 1)


def send(source, target, sent, got, where):
    copy = pltpu.make_async_remote_copy(
        src_ref=source, dst_ref=target, send_sem=sent, recv_sem=got, device_id=where, device_id_type=MESH
    )
    copy.start()
    return copy


def fetch_kernel(start_ref, middle_ref, tiles_ref, window, chosen, row_sent, row_got, band_sent, band_got):
    here, peers = band_peers()
    meet(peers)
    own = middle_ref.at[1, pl.ds(pl.multiple_of(here * QUARTER, QUARTER), QUARTER)]
    copies = [
        send(own, window.at[o + BAND_REACH], row_sent.at[n], row_got.at[n], {"rows": row_peer(-o)})
        for n, o in enumerate(OFFSETS)
    ]
    window[BAND_REACH] = own[...]
    for copy in copies:
        copy.wait()
    start = start_ref[0]
    copies = []
    for d in (2, 1, 3, 0):
        for j in range(2):
            offset = start + j * BANDS + peers[d]
            place = jnp.minimum(offset + BAND_REACH, 2 * BAND_REACH)
            tile = jnp.where(in_frame(offset), window[place].astype(F32), 0.0).astype(BF16)
            if d == 0:
                tiles_ref[j, here] = tile
            else:
                chosen[d, j] = tile
        if d:
            copies.append(
                send(chosen.at[d], tiles_ref.at[:, here], band_sent.at[d], band_got.at[d], {"band": peers[d]})
            )
    for copy in copies:
        copy.wait()


def fetch(start, middle):
    return pl.pallas_call(
        fetch_kernel,
        in_specs=[pl.BlockSpec(memory_space=pltpu.SMEM), pl.BlockSpec(memory_space=pltpu.VMEM)],
        out_specs=pl.BlockSpec(memory_space=pltpu.VMEM),
        out_shape=jax.ShapeDtypeStruct((2, BANDS, QUARTER, MID), BF16),
        scratch_shapes=[
            pltpu.VMEM((2 * BAND_REACH + 1, QUARTER, MID), BF16),
            pltpu.VMEM((BANDS, 2, QUARTER, MID), BF16),
            pltpu.SemaphoreType.DMA((len(OFFSETS),)),
            pltpu.SemaphoreType.DMA((len(OFFSETS),)),
            pltpu.SemaphoreType.DMA((BANDS,)),
            pltpu.SemaphoreType.DMA((BANDS,)),
        ],
        compiler_params=pltpu.CompilerParams(collective_id=1, has_side_effects=True),
    )(start, middle)


def combine_kernel(
    start_ref, terms_ref, share_ref, proj_ref, source_ref, target_ref, slots, shares, stage, landed, wide, wides, row_sent, row_got, band_sent, band_got
):
    here, peers = band_peers()
    meet(peers)
    term_copies, share_copies, copies = [], [], []
    for d in (2, 1, 3):
        where = {"band": peers[d]}
        term_copies.append(send(terms_ref.at[peers[d]], slots.at[here], band_sent.at[0, d], band_got.at[0, d], where))
    for d in (2, 1, 3):
        where = {"band": peers[d]}
        share_copies.append(send(share_ref.at[peers[d]], shares.at[here], band_sent.at[1, d], band_got.at[1, d], where))
    slots[here] = terms_ref[here]
    shares[here] = share_ref[here]
    for copy in term_copies:
        copy.wait()
    start = start_ref[0]

    def picked(o):
        slot = o - start
        place = jnp.clip(slot, 0, 7)
        tile = slots[lax.rem(place, BANDS), lax.div(place, BANDS)].astype(F32)
        return jnp.where((slot >= 0) & (slot < 8), tile, 0.0)

    for n, o in enumerate(OFFSETS):
        stage[n] = picked(o).astype(BF16)
        copies.append(send(stage.at[n], landed.at[n], row_sent.at[n], row_got.at[n], {"rows": row_peer(o)}))
    summed = picked(0)
    for copy in share_copies:
        copy.wait()
    total = shares[0].astype(F32)
    for q in range(1, BANDS):
        total = total + shares[q].astype(F32)
    source_ref[0] = total[:, :256]
    source_ref[1] = total[:, 256:]
    for copy in copies:
        copy.wait()
    for n, o in enumerate(OFFSETS):
        summed = summed + jnp.where(in_frame(-o), landed[n].astype(F32), 0.0)
    high, low = halves(summed)
    proj = proj_ref[...]
    full = dot(proj, high, 0, 1) + dot(proj, low, 0, 1)
    for q in range(BANDS):
        wide[q] = full[q * SHARE : (q + 1) * SHARE]
    copies = [
        send(wide.at[peers[d]], wides.at[here], band_sent.at[2, d], band_got.at[2, d], {"band": peers[d]})
        for d in (2, 1, 3)
    ]
    wides[here] = wide[here]
    for copy in copies:
        copy.wait()
    for q in range(BANDS):
        target_ref[q // 2, :, (q % 2) * QUARTER : (q % 2 + 1) * QUARTER] = wides[q]


def combine(start, terms, share, proj):
    vmem = pl.BlockSpec(memory_space=pltpu.VMEM)
    return pl.pallas_call(
        combine_kernel,
        in_specs=[pl.BlockSpec(memory_space=pltpu.SMEM), vmem, vmem, vmem],
        out_specs=[vmem, vmem],
        out_shape=[jax.ShapeDtypeStruct((ROWS_DEV, SHARE, PIXELS // ROWS_DEV), F32)] * 2,
        scratch_shapes=[
            pltpu.VMEM((BANDS, 2, QUARTER, MID), BF16),
            pltpu.VMEM((BANDS, SHARE, PIXELS), BF16),
            pltpu.VMEM((len(OFFSETS), QUARTER, MID), BF16),
            pltpu.VMEM((len(OFFSETS), QUARTER, MID), BF16),
            pltpu.VMEM((BANDS, SHARE, QUARTER), F32),
            pltpu.VMEM((BANDS, SHARE, QUARTER), F32),
            pltpu.SemaphoreType.DMA((len(OFFSETS),)),
            pltpu.SemaphoreType.DMA((len(OFFSETS),)),
            pltpu.SemaphoreType.DMA((3, BANDS)),
            pltpu.SemaphoreType.DMA((3, BANDS)),
        ],
        compiler_params=pltpu.CompilerParams(collective_id=2, has_side_effects=True),
    )(start, terms, share, proj)


def shards(frames, conv_weight, proj_weight, band_start, band_count, pyramid_grad):
    rim_row = shifted(frames[:, -1:], "rows", 1)
    convolved = lax.conv_general_dilated(
        jnp.concatenate([rim_row, frames], axis=1),
        conv_weight,
        (2, 2),
        ((0, 0), (1, 0)),
        dimension_numbers=("NHWC", "HWIO", "NHWC"),
        preferred_element_type=F32,
    )
    middle = jax.nn.relu(convolved).astype(BF16).reshape(2, PIXELS, MID)
    target = fetch(band_start, middle).reshape(2, PIXELS, MID)
    pyramid, terms, share = tiles(band_count, middle[0], target, jnp.swapaxes(pyramid_grad, 3, 4), proj_weight)
    source_share, target_share = combine(band_start, terms, share, proj_weight)
    return jnp.swapaxes(pyramid, 3, 4), jnp.swapaxes(source_share, 1, 2), jnp.swapaxes(target_share, 1, 2)


def solution(mesh):
    in_specs = (
        P(None, "rows", None, None),
        P(),
        P(),
        P("rows"),
        P("rows"),
        P("rows", None, "band", None, None),
    )
    out_specs = (
        P("rows", None, "band", None, None),
        P("rows", None, "band"),
        P("rows", None, "band"),
    )
    return jax.shard_map(shards, mesh=mesh, in_specs=in_specs, out_specs=out_specs, check_vma=False)
```

time: 149 us -> 73.8 us (0.50)
  the two profiles are of different devices: /device:TPU:256 before, /device:TPU:1 now
where the time goes in v2:
time: 73.8 us; the launch traced here: 73.4 us
  Pallas kernels  53.8 us (73%)
  local copies, waits for them, and re-layouts  7.2 us (10%)
  starting transfers between devices  4.58 us (6%)
  waiting for transfers between devices  3.26 us (4%)
  matrix products  2.59 us (4%)
  between operations  1.99 us (3%)
    pallas_call x1, Pallas kernels, fetch(): pl.pallas_call(fetch_kernel, in_specs=[pl.BlockSpec(memory_space=pltpu.SM...  23.9 us
    pallas_call x1, Pallas kernels, combine(): pl.pallas_call(combine_kernel, in_specs=[pl.BlockSpec(memory_space=pltpu....  23.3 us
    pallas_call x1, Pallas kernels, tiles(): pl.pallas_call(tile_kernel, grid=(2,), in_specs=[pl.BlockSpec(memory_spac...  6.58 us
    unnamed x6, local copies, waits for them, and re-layouts  6.28 us
    ppermute x1, starting transfers between devices, shifted(): return lax.ppermute(x, axis, pairs)  4.58 us
    ppermute x1, waiting for transfers between devices, shifted(): return lax.ppermute(x, axis, pairs)  3.26 us
    conv_general_dilated x1, matrix products, shards(): lax.conv_general_dilated(jnp.concatenate([rim_row, frames], axis=1), conv...  2.59 us
  transfers between devices with their start and end apart: 1, of which 1 were waited for; matrix products, arithmetic and copies ran while one was open for 0% of the time, Pallas kernels for 0%

profile of v2, /device:TPU:1, one launch (start us, length us, event | category | flops | bytes accessed | tf_op | source)
XLA Modules:
  0.0 73.4 jit_solution(16686448733002306526)
XLA Ops:
  0.6 0.0 copy-start
  0.6 2.5 %copy.12 = bf16[2,4,512,96]{3,0,2,1:T(2,128)(2,1)S(1)} copy(bf16[2,4,512,96]{2,3,1,0:T(8,128)(2,1)} %param.6) | data formatting | bytes 1572864 | tf_op args[0]
  3.1 0.2 slice.9
  3.3 4.6 %collective-permute-start = (bf16[2,1,512,96]{3,0,2,1:T(2,128)(2,1)S(1)}, bf16[2,1,512,96]{3,0,2,1:T(2,128)(2,1)S(1)}, u32[]{:S(2)}, u32[]{:S(2)}) collective-permute-start(bf16[2,1,512,96]{3,0,2,1:T(2,128)(2,1)S(1)} %slice.9), channel_id=1, source_target_pairs={{0,4},{4,8},{8,12},{12,16},{16,20},{20,24},{24,28},{28,32},{32,36}... | collective-permute-start | bytes 589832 | tf_op jit(solution)/shard_map/ppermute | solution.py:26
  9.2 3.3 %collective-permute-done = bf16[2,1,512,96]{3,0,2,1:T(2,128)(2,1)S(1)} collective-permute-done((bf16[2,1,512,96]{3,0,2,1:T(2,128)(2,1)S(1)}, bf16[2,1,512,96]{3,0,2,1:T(2,128)(2,1)S(1)}, u32[]{:S(2)}, u32[]{:S(2)}) %collective-permute-start) | collective-permute-done | bytes 196640 | tf_op jit(solution)/shard_map/ppermute | solution.py:26
  12.4 0.0 copy-done
  12.5 2.6 %fusion.2 = bf16[2,2,256,128]{3,0,2,1:T(2,128)(2,1)S(1)} fusion(bf16[3,3,96,128]{3,2,1,0:T(8,128)(2,1)S(1)} %copy-done, bf16[2,4,512,96]{3,0,2,1:T(2,128)(2,1)S(1)} %copy.12, bf16[2,1,512,96]{3,0,2,1:T(2,128)(2,1)S(1)} %collective-permute-done), kind=kOutput, calls=%fused_computation.3 | convolution fusion | flops 228425728 | bytes 1466368 | tf_op jit(solution)/shard_map/conv_general_dilated | solution.py:280
  15.0 0.7 %copy.14 = bf16[2,2,256,128]{3,2,1,0:T(8,128)(2,1)} copy(bf16[2,2,256,128]{3,0,2,1:T(2,128)(2,1)S(1)} %fusion.2) | data formatting | bytes 524288 | tf_op jit(solution)/shard_map/convert_element_type | solution.py:288
  15.8 0.7 copy.15
  16.5 23.9 %shard_map.85 = bf16[2,4,128,128]{3,2,1,0:T(8,128)(2,1)} custom-call(s32[1]{0:T(128)S(6)} %copy.18.start_ref, bf16[2,512,128]{2,1,0:T(8,128)(2,1)} %bitcast.10), custom_call_target="tpu_custom_call" | custom-call | tf_op jit(solution)/shard_map/pallas_call | solution.py:183
  40.4 6.6 %shard_map.86 = (bf16[1,2,1,960,512]{4,3,2,1,0:T(8,128)(2,1)}, bf16[4,2,128,128]{3,2,1,0:T(8,128)(2,1)}, bf16[4,64,512]{2,1,0:T(8,128)(2,1)}) custom-call(s32[1]{0:T(128)S(6)} %copy.19.count_ref, bf16[512,128]{1,0:T(8,128)(2,1)} %bitcast.13, bf16[2,512,128]{2,1,0:T(8,128)(2,1)} %bitcast.12, bf16[1,2,1,960,512]{4,3,2,1,0:T(8,128)(2,1)} %bitcast.9, ...), custom_call_target="tpu_custom_call" | custom-call | tf_op jit(solution)/shard_map/pallas_call | solution.py:91
  47.0 23.3 %shard_map.87 = (f32[2,64,256]{2,1,0:T(8,128)}, f32[2,64,256]{2,1,0:T(8,128)}) custom-call(s32[1]{0:T(128)S(6)} %copy.18.start_ref, bf16[4,2,128,128]{3,2,1,0:T(8,128)(2,1)} %get-tuple-element.9.terms_ref, bf16[4,64,512]{2,1,0:T(8,128)(2,1)} %get-tuple-element.10.share_ref, bf16[128,256]{1,0:T(8,128)(2,1)} %proj_ref.3), custom_call_target="tpu_custom_call" | custom-call | tf_op jit(solution)/shard_map/pallas_call | solution.py:257
  70.3 1.6 %copy.20 = f32[2,256,64]{1,2,0:T(8,128)} copy(f32[2,256,64]{1,2,0:T(8,128)} %bitcast.15) | data formatting | bytes 262144
  71.9 1.6 %copy.21 = f32[2,256,64]{1,2,0:T(8,128)} copy(f32[2,256,64]{1,2,0:T(8,128)} %bitcast.14) | data formatting | bytes 262144
Async XLA Ops:
  0.6 11.8 %copy-start = (bf16[3,3,96,128]{3,2,1,0:T(8,128)(2,1)S(1)}, bf16[3,3,96,128]{3,2,1,0:T(8,128)(2,1)}, u32[]{:S(2)}) copy-start(bf16[3,3,96,128]{3,2,1,0:T(8,128)(2,1)} %param.7) | copy-start | bytes 663556
  3.3 9.1 %collective-permute-start = (bf16[2,1,512,96]{3,0,2,1:T(2,128)(2,1)S(1)}, bf16[2,1,512,96]{3,0,2,1:T(2,128)(2,1)S(1)}, u32[]{:S(2)}, u32[]{:S(2)}) collective-permute-start(bf16[2,1,512,96]{3,0,2,1:T(2,128)(2,1)S(1)} %slice.9), channel_id=1, source_target_pairs={{0,4},{4,8},{8,12},{12,16},{16,20},{20,24},{24,28},{28,32},{32,36}... | collective-permute-start | bytes 589832 | tf_op jit(solution)/shard_map/ppermute | solution.py:26

commit v3 on v2

--- a/solution.py
+++ b/solution.py
@@ -18,12 +18,6 @@
 BF16 = jnp.bfloat16
 MESH = pl.DeviceIdType.MESH
 OFFSETS = (-4, 4, -3, 3, -2, 2, -1, 1)
-
-
-def shifted(x, axis, by):
-    size = lax.axis_size(axis)
-    pairs = [(i, i + by) for i in range(size) if 0 <= i + by < size]
-    return lax.ppermute(x, axis, pairs)
 
 
 def halves(x):
@@ -138,7 +132,7 @@
         pl.semaphore_signal(barrier, inc=1, device_id={"rows": row_peer(o)}, device_id_type=MESH)
     for d in range(1, BANDS):
         pl.semaphore_signal(barrier, inc=1, device_id={"band": peers[d]}, device_id_type=MESH)
-    pl.semaphore_wait(barrier, len(OFFSETS) + BANDS - 1)
+    return barrier
 
 
 def send(source, target, sent, got, where):
@@ -149,14 +143,40 @@
     return copy
 
 
-def fetch_kernel(start_ref, middle_ref, tiles_ref, window, chosen, row_sent, row_got, band_sent, band_got):
+def fetch_kernel(
+    start_ref, frames_ref, conv_ref, tiles_ref, source_ref, rim, middle, taps, window, chosen, rim_sent, rim_got, row_sent, row_got, band_sent, band_got
+):
     here, peers = band_peers()
-    meet(peers)
-    own = middle_ref.at[1, pl.ds(pl.multiple_of(here * QUARTER, QUARTER), QUARTER)]
+    barrier = meet(peers)
+    weight = jnp.concatenate([conv_ref[:, dx].reshape(3 * 96, MID) for dx in range(3)], axis=1)
+
+    def convolve(stack, out, r):
+        full = dot(stack, weight, 0, 0)
+        for dx in range(3):
+            taps[dx, 8 : 8 + PIXELS] = full[:, dx * MID : (dx + 1) * MID]
+        total = taps[0, pl.ds(7, 256, stride=2)] + taps[1, pl.ds(8, 256, stride=2)] + taps[2, pl.ds(9, 256, stride=2)]
+        out[r * 256 : (r + 1) * 256] = jnp.maximum(total, 0.0).astype(BF16)
+
+    def first_row(f):
+        above = jnp.where(in_frame(-1), rim[f].astype(F32), 0.0).astype(BF16)
+        return jnp.concatenate([above, frames_ref[f, 0], frames_ref[f, 1]], axis=0)
+
+    taps[0, :8] = jnp.zeros((8, MID), F32)
+    convolve(frames_ref[1, 1:4].reshape(3 * 96, PIXELS), middle, 1)
+    pl.semaphore_wait(barrier, len(OFFSETS) + BANDS - 1)
+    rims = [
+        send(frames_ref.at[f, 3], rim.at[f], rim_sent.at[f], rim_got.at[f], {"rows": row_peer(1)}) for f in (1, 0)
+    ]
+    convolve(frames_ref[0, 1:4].reshape(3 * 96, PIXELS), source_ref, 1)
+    rims[0].wait()
+    convolve(first_row(1), middle, 0)
+    own = middle.at[pl.ds(pl.multiple_of(here * QUARTER, QUARTER), QUARTER)]
     copies = [
         send(own, window.at[o + BAND_REACH], row_sent.at[n], row_got.at[n], {"rows": row_peer(-o)})
         for n, o in enumerate(OFFSETS)
     ]
+    rims[1].wait()
+    convolve(first_row(0), source_ref, 0)
     window[BAND_REACH] = own[...]
     for copy in copies:
         copy.wait()
@@ -179,29 +199,38 @@
         copy.wait()
 
 
-def fetch(start, middle):
+def fetch(start, frames, conv):
+    vmem = pl.BlockSpec(memory_space=pltpu.VMEM)
     return pl.pallas_call(
         fetch_kernel,
-        in_specs=[pl.BlockSpec(memory_space=pltpu.SMEM), pl.BlockSpec(memory_space=pltpu.VMEM)],
-        out_specs=pl.BlockSpec(memory_space=pltpu.VMEM),
-        out_shape=jax.ShapeDtypeStruct((2, BANDS, QUARTER, MID), BF16),
+        in_specs=[pl.BlockSpec(memory_space=pltpu.SMEM), vmem, vmem],
+        out_specs=[vmem, vmem],
+        out_shape=[
+            jax.ShapeDtypeStruct((2, BANDS, QUARTER, MID), BF16),
+            jax.ShapeDtypeStruct((PIXELS, MID), BF16),
+        ],
         scratch_shapes=[
+            pltpu.VMEM((2, 96, PIXELS), BF16),
+            pltpu.VMEM((PIXELS, MID), BF16),
+            pltpu.VMEM((3, PIXELS + 16, MID), F32),
             pltpu.VMEM((2 * BAND_REACH + 1, QUARTER, MID), BF16),
             pltpu.VMEM((BANDS, 2, QUARTER, MID), BF16),
+            pltpu.SemaphoreType.DMA((2,)),
+            pltpu.SemaphoreType.DMA((2,)),
             pltpu.SemaphoreType.DMA((len(OFFSETS),)),
             pltpu.SemaphoreType.DMA((len(OFFSETS),)),
             pltpu.SemaphoreType.DMA((BANDS,)),
             pltpu.SemaphoreType.DMA((BANDS,)),
         ],
         compiler_params=pltpu.CompilerParams(collective_id=1, has_side_effects=True),
-    )(start, middle)
+    )(start, frames, conv)
 
 
 def combine_kernel(
-    start_ref, terms_ref, share_ref, proj_ref, source_ref, target_ref, slots, shares, stage, landed, wide, wides, row_sent, row_got, band_sent, band_got
+    start_ref, terms_ref, share_ref, proj_ref, source_ref, wides, slots, shares, stage, landed, wide, row_sent, row_got, band_sent, band_got
 ):
     here, peers = band_peers()
-    meet(peers)
+    pl.semaphore_wait(meet(peers), len(OFFSETS) + BANDS - 1)
     term_copies, share_copies, copies = [], [], []
     for d in (2, 1, 3):
         where = {"band": peers[d]}
@@ -248,8 +277,6 @@
     wides[here] = wide[here]
     for copy in copies:
         copy.wait()
-    for q in range(BANDS):
-        target_ref[q // 2, :, (q % 2) * QUARTER : (q % 2 + 1) * QUARTER] = wides[q]
 
 
 def combine(start, terms, share, proj):
@@ -258,14 +285,16 @@
         combine_kernel,
         in_specs=[pl.BlockSpec(memory_space=pltpu.SMEM), vmem, vmem, vmem],
         out_specs=[vmem, vmem],
-        out_shape=[jax.ShapeDtypeStruct((ROWS_DEV, SHARE, PIXELS // ROWS_DEV), F32)] * 2,
+        out_shape=[
+            jax.ShapeDtypeStruct((ROWS_DEV, SHARE, PIXELS // ROWS_DEV), F32),
+            jax.ShapeDtypeStruct((BANDS, SHARE, QUARTER), F32),
+        ],
         scratch_shapes=[
             pltpu.VMEM((BANDS, 2, QUARTER, MID), BF16),
             pltpu.VMEM((BANDS, SHARE, PIXELS), BF16),
             pltpu.VMEM((len(OFFSETS), QUARTER, MID), BF16),
             pltpu.VMEM((len(OFFSETS), QUARTER, MID), BF16),
             pltpu.VMEM((BANDS, SHARE, QUARTER), F32),
-            pltpu.VMEM((BANDS, SHARE, QUARTER), F32),
             pltpu.SemaphoreType.DMA((len(OFFSETS),)),
             pltpu.SemaphoreType.DMA((len(OFFSETS),)),
             pltpu.SemaphoreType.DMA((3, BANDS)),
@@ -275,20 +304,27 @@
     )(start, terms, share, proj)
 
 
+def finish_kernel(summed_ref, wides_ref, source_ref, target_ref):
+    source_ref[...] = summed_ref[...]
+    for q in range(BANDS):
+        target_ref[q // 2, :, (q % 2) * QUARTER : (q % 2 + 1) * QUARTER] = wides_ref[q]
+
+
+def finish(summed, wides):
+    vmem = pl.BlockSpec(memory_space=pltpu.VMEM)
+    return pl.pallas_call(
+        finish_kernel,
+        in_specs=[vmem, vmem],
+        out_specs=[vmem, vmem],
+        out_shape=[jax.ShapeDtypeStruct((ROWS_DEV, SHARE, PIXELS // ROWS_DEV), F32)] * 2,
+    )(summed, wides)
+
+
 def shards(frames, conv_weight, proj_weight, band_start, band_count, pyramid_grad):
-    rim_row = shifted(frames[:, -1:], "rows", 1)
-    convolved = lax.conv_general_dilated(
-        jnp.concatenate([rim_row, frames], axis=1),
-        conv_weight,
-        (2, 2),
-        ((0, 0), (1, 0)),
-        dimension_numbers=("NHWC", "HWIO", "NHWC"),
-        preferred_element_type=F32,
-    )
-    middle = jax.nn.relu(convolved).astype(BF16).reshape(2, PIXELS, MID)
-    target = fetch(band_start, middle).reshape(2, PIXELS, MID)
-    pyramid, terms, share = tiles(band_count, middle[0], target, jnp.swapaxes(pyramid_grad, 3, 4), proj_weight)
-    source_share, target_share = combine(band_start, terms, share, proj_weight)
+    target, source = fetch(band_start, jnp.swapaxes(frames, 2, 3), conv_weight)
+    target = target.reshape(2, PIXELS, MID)
+    pyramid, terms, share = tiles(band_count, source, target, jnp.swapaxes(pyramid_grad, 3, 4), proj_weight)
+    source_share, target_share = finish(*combine(band_start, terms, share, proj_weight))
     return jnp.swapaxes(pyramid, 3, 4), jnp.swapaxes(source_share, 1, 2), jnp.swapaxes(target_share, 1, 2)
 
 

time: 73.8 us -> 61.8 us (0.84)
  local copies, waits for them, and re-layouts: 7.2 us -> 0 us
  Pallas kernels: 53.8 us -> 59.6 us
  starting transfers between devices: 4.58 us -> 0 us
  waiting for transfers between devices: 3.26 us -> 0 us
  matrix products: 2.59 us -> 0 us
    pallas_call x1, Pallas kernels: 23.9 us -> 30.5 us  [fetch(): pl.pallas_call(fetch_kernel, in_specs=[pl.BlockSpec(memory_space=pltpu.SM...]
    unnamed x6 -> x0, local copies, waits for them, and re-layouts: 6.28 us -> none
    ppermute x1 -> x0, starting transfers between devices: 4.58 us -> none  [shifted(): return lax.ppermute(x, axis, pairs)]
    ppermute x1 -> x0, waiting for transfers between devices: 3.26 us -> none  [shifted(): return lax.ppermute(x, axis, pairs)]
    conv_general_dilated x1 -> x0, matrix products: 2.59 us -> none  [shards(): lax.conv_general_dilated(jnp.concatenate([rim_row, frames], axis=1), conv...]
    pallas_call x1, Pallas kernels: 23.3 us -> 20.8 us  [combine(): pl.pallas_call(combine_kernel, in_specs=[pl.BlockSpec(memory_space=pltpu....]
    pallas_call x0 -> x1, Pallas kernels: none -> 1.68 us  [finish(): pl.pallas_call(finish_kernel, in_specs=[vmem, vmem], out_specs=[vmem, vme...]
    convert_element_type x1 -> x0, local copies, waits for them, and re-layouts: 0.74 us -> none  [shards(): middle = jax.nn.relu(convolved).astype(BF16).reshape(2, PIXELS, MID)]
  transfers between devices with their start and end apart: 1 -> 0, of which waited for: 1 -> 0; matrix products, arithmetic and copies ran while one was open for 0% -> 0% of each run, Pallas kernels for 0% -> 0%
where the time goes in v3:
time: 61.8 us; the launch traced here: 61.5 us
  Pallas kernels  59.6 us (96%)
  between operations  1.94 us (3%)
    pallas_call x1, Pallas kernels, fetch(): pl.pallas_call(fetch_kernel, in_specs=[pl.BlockSpec(memory_space=pltpu.SM...  30.5 us
    pallas_call x1, Pallas kernels, combine(): pl.pallas_call(combine_kernel, in_specs=[pl.BlockSpec(memory_space=pltpu....  20.8 us
    pallas_call x1, Pallas kernels, tiles(): pl.pallas_call(tile_kernel, grid=(2,), in_specs=[pl.BlockSpec(memory_spac...  6.59 us
    pallas_call x1, Pallas kernels, finish(): pl.pallas_call(finish_kernel, in_specs=[vmem, vmem], out_specs=[vmem, vme...  1.68 us

profile of v3, /device:TPU:1, one launch (start us, length us, event | category | flops | bytes accessed | tf_op | source)
XLA Modules:
  0.0 61.5 jit_solution(76894242059687261)
XLA Ops:
  1.9 30.5 %shard_map.85 = (bf16[2,4,128,128]{3,2,1,0:T(8,128)(2,1)}, bf16[512,128]{1,0:T(8,128)(2,1)}) custom-call(s32[1]{0:T(128)S(6)} %copy.9.start_ref, bf16[2,4,96,512]{3,2,1,0:T(8,128)(2,1)} %bitcast.7, bf16[3,3,96,128]{3,2,1,0:T(8,128)(2,1)} %conv_ref.1), custom_call_target="tpu_custom_call" | custom-call | tf_op jit(solution)/shard_map/pallas_call | solution.py:204
  32.4 6.6 %shard_map.86 = (bf16[1,2,1,960,512]{4,3,2,1,0:T(8,128)(2,1)}, bf16[4,2,128,128]{3,2,1,0:T(8,128)(2,1)}, bf16[4,64,512]{2,1,0:T(8,128)(2,1)}) custom-call(s32[1]{0:T(128)S(6)} %copy.10.count_ref, bf16[512,128]{1,0:T(8,128)(2,1)} %get-tuple-element.12.source_ref, bf16[2,512,128]{2,1,0:T(8,128)(2,1)} %bitcast.8, bf16[1,2,1,960,512]{4,3,2,1,0:T(8,128)(2,1)} %bitcast.6, ...), custom_call_target="tpu_custom_call" | custom-call | tf_op jit(solution)/shard_map/pallas_call | solution.py:85
  39.0 20.8 %shard_map.87 = (f32[2,64,256]{2,1,0:T(8,128)}, f32[4,64,128]{2,1,0:T(8,128)}) custom-call(s32[1]{0:T(128)S(6)} %copy.9.start_ref, bf16[4,2,128,128]{3,2,1,0:T(8,128)(2,1)} %get-tuple-element.15.terms_ref, bf16[4,64,512]{2,1,0:T(8,128)(2,1)} %get-tuple-element.16.share_ref, bf16[128,256]{1,0:T(8,128)(2,1)} %proj_ref.3), custom_call_target="tpu_custom_call" | custom-call | tf_op jit(solution)/shard_map/pallas_call | solution.py:284
  59.8 1.7 %shard_map.88 = (f32[2,64,256]{2,1,0:T(8,128)}, f32[2,64,256]{2,1,0:T(8,128)}) custom-call(f32[2,64,256]{2,1,0:T(8,128)} %get-tuple-element.17.summed_ref, f32[4,64,128]{2,1,0:T(8,128)} %get-tuple-element.18.wides_ref), custom_call_target="tpu_custom_call" | custom-call | tf_op jit(solution)/shard_map/pallas_call | solution.py:315

commit v4 on v3

v4 whole, which is shorter than its diff:
```python
import jax
import jax.numpy as jnp
from jax import lax
from jax.experimental import pallas as pl
from jax.experimental.pallas import tpu as pltpu
from jax.sharding import PartitionSpec as P

ROWS_DEV = 2
BAND_REACH = 4
PIXELS = 512
MID = 128
LOWER = 448
BANDS = 4
QUARTER = PIXELS // BANDS
SHARE = 64
SCALE = 1.0 / 16.0
F32 = jnp.float32
BF16 = jnp.bfloat16
MESH = pl.DeviceIdType.MESH
OFFSETS = (-4, 4, -3, 3, -2, 2, -1, 1)


def halves(x):
    high = x.astype(BF16)
    return high, (x - high.astype(F32)).astype(BF16)


def dot(a, b, da=1, db=0):
    return lax.dot_general(a, b, (((da,), (db,)), ((), ())), preferred_element_type=F32)


def pooling(shape, pixel_axis):
    pixel = lax.broadcasted_iota(jnp.int32, shape, pixel_axis)
    group = lax.broadcasted_iota(jnp.int32, shape, 1 - pixel_axis)
    shift = jnp.where(group < 256, 1, jnp.where(group < 384, 2, 3))
    first = jnp.where(group < 256, 0, jnp.where(group < 384, 256, 384))
    weight = jnp.where(group < 256, 0.5, jnp.where(group < 384, 0.25, 0.125))
    return jnp.where((pixel >> shift) == group - first, weight, 0.0).astype(BF16)


def tile_kernel(count_ref, source_ref, target_ref, proj_ref, summed_ref, wides_ref, pyramid_ref, sg_ref, tg_ref, pool, pair):
    j = pl.program_id(0)

    @pl.when(j == 0)
    def _():
        source = source_ref[...]
        pool[...] = pooling((LOWER, PIXELS), 1)
        square_high, square_low = halves(dot(proj_ref[...], proj_ref[...], 1, 1) * SCALE)
        high, low = halves(dot(source, square_high) + dot(source, square_low))
        pair[...] = jnp.concatenate([high, low], axis=1)
        sg_ref[...] = summed_ref[...]
        for q in range(BANDS):
            tg_ref[q // 2, :, (q % 2) * QUARTER : (q % 2 + 1) * QUARTER] = wides_ref[q]

    valid = j * BANDS + lax.axis_index("band") < count_ref[0]
    target = target_ref[0]
    high, low = halves(dot(pool[...], target))
    base = dot(jnp.concatenate([target, target], axis=1), pair[...], 1, 1)
    rest = dot(jnp.concatenate([high, high], axis=1), pair[...], 1, 1) + dot(low, pair[:, :MID], 1, 1)
    pyramid_ref[0, 0, 0, :PIXELS] = jnp.where(valid, base, 0.0).astype(BF16)
    pyramid_ref[0, 0, 0, PIXELS:] = jnp.where(valid, rest, 0.0).astype(BF16)


def tiles(count, source, target, proj, summed, wides):
    share = (ROWS_DEV, SHARE, PIXELS // ROWS_DEV)
    return pl.pallas_call(
        tile_kernel,
        grid=(2,),
        in_specs=[
            pl.BlockSpec(memory_space=pltpu.SMEM),
            pl.BlockSpec((PIXELS, MID), lambda j: (0, 0)),
            pl.BlockSpec((1, PIXELS, MID), lambda j: (j, 0, 0)),
            pl.BlockSpec((MID, 256), lambda j: (0, 0)),
            pl.BlockSpec(share, lambda j: (0, 0, 0)),
            pl.BlockSpec((BANDS, SHARE, QUARTER), lambda j: (0, 0, 0)),
        ],
        out_specs=[
            pl.BlockSpec((1, 1, 1, 960, PIXELS), lambda j: (0, j, 0, 0, 0)),
            pl.BlockSpec(share, lambda j: (0, 0, 0)),
            pl.BlockSpec(share, lambda j: (0, 0, 0)),
        ],
        out_shape=[
            jax.ShapeDtypeStruct((1, 2, 1, 960, PIXELS), BF16),
            jax.ShapeDtypeStruct(share, F32),
            jax.ShapeDtypeStruct(share, F32),
        ],
        scratch_shapes=[pltpu.VMEM((LOWER, PIXELS), BF16), pltpu.VMEM((PIXELS, 2 * MID), BF16)],
    )(count, source, target, proj, summed, wides)


def band_peers():
    here = lax.axis_index("band")
    return here, [lax.rem(here + d, BANDS) for d in range(BANDS)]


def row_peer(offset):
    size = lax.axis_size("rows")
    return lax.rem(lax.axis_index("rows") + offset + size, size)


def in_frame(offset):
    block = lax.axis_index("rows") + offset
    return (block >= 0) & (block < lax.axis_size("rows"))


def meet(peers):
    barrier = pltpu.get_barrier_semaphore()
    for o in OFFSETS:
        pl.semaphore_signal(barrier, inc=1, device_id={"rows": row_peer(o)}, device_id_type=MESH)
    for d in range(1, BANDS):
        pl.semaphore_signal(barrier, inc=1, device_id={"band": peers[d]}, device_id_type=MESH)
    return barrier


def send(source, target, sent, got, where):
    copy = pltpu.make_async_remote_copy(
        src_ref=source, dst_ref=target, send_sem=sent, recv_sem=got, device_id=where, device_id_type=MESH
    )
    copy.start()
    return copy


def fetch_kernel(
    start_ref, count_ref, frames_ref, conv_ref, proj_ref, grad_ref, tiles_ref, source_ref, summed_ref, wides,
    rim, middle, taps, window, chosen, spread, pool, terms, slots, share, shares, stage, landed, wide,
    rim_sent, rim_got, row_sent, row_got, band_sent, band_got
):
    here, peers = band_peers()
    barrier = meet(peers)
    weight = jnp.concatenate([conv_ref[:, dx].reshape(3 * 96, MID) for dx in range(3)], axis=1)

    def convolve(stack, out, r):
        full = dot(stack, weight, 0, 0)
        for dx in range(3):
            taps[dx, 8 : 8 + PIXELS] = full[:, dx * MID : (dx + 1) * MID]
        total = taps[0, pl.ds(7, 256, stride=2)] + taps[1, pl.ds(8, 256, stride=2)] + taps[2, pl.ds(9, 256, stride=2)]
        out[r * 256 : (r + 1) * 256] = jnp.maximum(total, 0.0).astype(BF16)

    def first_row(f):
        above = jnp.where(in_frame(-1), rim[f].astype(F32), 0.0).astype(BF16)
        return jnp.concatenate([above, frames_ref[f, 0], frames_ref[f, 1]], axis=0)

    taps[0, :8] = jnp.zeros((8, MID), F32)
    convolve(frames_ref[1, 1:4].reshape(3 * 96, PIXELS), middle, 1)
    pl.semaphore_wait(barrier, len(OFFSETS) + BANDS - 1)
    rims = [
        send(frames_ref.at[f, 3], rim.at[f], rim_sent.at[f], rim_got.at[f], {"rows": row_peer(1)}) for f in (1, 0)
    ]
    convolve(frames_ref[0, 1:4].reshape(3 * 96, PIXELS), source_ref, 1)
    spread[...] = pooling((PIXELS, LOWER), 0)
    pool[...] = pooling((LOWER, PIXELS), 1)
    rims[0].wait()
    convolve(first_row(1), middle, 0)
    own = middle.at[pl.ds(pl.multiple_of(here * QUARTER, QUARTER), QUARTER)]
    copies = [
        send(own, window.at[o + BAND_REACH], row_sent.at[0, n], row_got.at[0, n], {"rows": row_peer(-o)})
        for n, o in enumerate(OFFSETS)
    ]
    rims[1].wait()
    convolve(first_row(0), source_ref, 0)
    window[BAND_REACH] = own[...]
    source = source_ref[...]
    for j in range(2):
        gathered = dot(grad_ref[0, j, 0], source)
        both = dot(spread[...], jnp.concatenate(halves(gathered[PIXELS:]), axis=1))
        term = (gathered[:PIXELS] + both[:, :MID] + both[:, MID:]) * SCALE
        term = jnp.where(j * BANDS + here < count_ref[0], term, 0.0).astype(BF16)
        for q in range(BANDS):
            terms[q, j] = term[q * QUARTER : (q + 1) * QUARTER]

    def across(kind, outgoing, incoming):
        return [
            send(outgoing.at[peers[d]], incoming.at[here], band_sent.at[kind, d], band_got.at[kind, d], {"band": peers[d]})
            for d in (2, 1, 3)
        ]

    term_copies = across(0, terms, slots)
    slots[here] = terms[here]
    for copy in copies:
        copy.wait()
    start = start_ref[0]
    tile_copies = []
    for d in (2, 1, 3, 0):
        for j in range(2):
            offset = start + j * BANDS + peers[d]
            place = jnp.minimum(offset + BAND_REACH, 2 * BAND_REACH)
            tile = jnp.where(in_frame(offset), window[place].astype(F32), 0.0).astype(BF16)
            if d == 0:
                tiles_ref[j, here] = tile
            else:
                chosen[d, j] = tile
        if d:
            tile_copies.append(
                send(chosen.at[d], tiles_ref.at[:, here], band_sent.at[1, d], band_got.at[1, d], {"band": peers[d]})
            )
    for copy in term_copies:
        copy.wait()

    def picked(o):
        slot = o - start
        place = jnp.clip(slot, 0, 7)
        tile = slots[lax.rem(place, BANDS), lax.div(place, BANDS)].astype(F32)
        return jnp.where((slot >= 0) & (slot < 8), tile, 0.0)

    copies = []
    for n, o in enumerate(OFFSETS):
        stage[n] = picked(o).astype(BF16)
        copies.append(send(stage.at[n], landed.at[n], row_sent.at[1, n], row_got.at[1, n], {"rows": row_peer(o)}))
    summed = picked(0)
    for copy in tile_copies:
        copy.wait()
    total = jnp.zeros((MID, PIXELS), F32)
    for j in range(2):
        target = tiles_ref[j].reshape(PIXELS, MID)
        lower = jnp.concatenate(halves(dot(pool[...], target)), axis=1)
        both = dot(lower, grad_ref[0, j, 0, PIXELS:], 0, 0)
        part = dot(target, grad_ref[0, j, 0, :PIXELS], 0, 0) + both[:MID] + both[MID:]
        total = total + jnp.where(j * BANDS + here < count_ref[0], part, 0.0)
    high, low = halves(total * SCALE)
    proj = proj_ref[...]
    full = dot(proj, high, 0, 0) + dot(proj, low, 0, 0)
    for q in range(BANDS):
        share[q] = full[q * SHARE : (q + 1) * SHARE].astype(BF16)
    share_copies = across(2, share, shares)
    shares[here] = share[here]
    for copy in copies:
        copy.wait()
    for n, o in enumerate(OFFSETS):
        summed = summed + jnp.where(in_frame(-o), landed[n].astype(F32), 0.0)
    high, low = halves(summed)
    full = dot(proj, high, 0, 1) + dot(proj, low, 0, 1)
    for q in range(BANDS):
        wide[q] = full[q * SHARE : (q + 1) * SHARE]
    wide_copies = across(3, wide, wides)
    wides[here] = wide[here]
    for copy in share_copies:
        copy.wait()
    total = shares[0].astype(F32)
    for q in range(1, BANDS):
        total = total + shares[q].astype(F32)
    summed_ref[0] = total[:, :256]
    summed_ref[1] = total[:, 256:]
    for copy in wide_copies:
        copy.wait()


def fetch(start, count, frames, conv, proj, grad):
    vmem = pl.BlockSpec(memory_space=pltpu.VMEM)
    smem = pl.BlockSpec(memory_space=pltpu.SMEM)
    return pl.pallas_call(
        fetch_kernel,
        in_specs=[smem, smem, vmem, vmem, vmem, vmem],
        out_specs=[vmem] * 4,
        out_shape=[
            jax.ShapeDtypeStruct((2, BANDS, QUARTER, MID), BF16),
            jax.ShapeDtypeStruct((PIXELS, MID), BF16),
            jax.ShapeDtypeStruct((ROWS_DEV, SHARE, PIXELS // ROWS_DEV), F32),
            jax.ShapeDtypeStruct((BANDS, SHARE, QUARTER), F32),
        ],
        scratch_shapes=[
            pltpu.VMEM((2, 96, PIXELS), BF16),
            pltpu.VMEM((PIXELS, MID), BF16),
            pltpu.VMEM((3, PIXELS + 16, MID), F32),
            pltpu.VMEM((2 * BAND_REACH + 1, QUARTER, MID), BF16),
            pltpu.VMEM((BANDS, 2, QUARTER, MID), BF16),
            pltpu.VMEM((PIXELS, LOWER), BF16),
            pltpu.VMEM((LOWER, PIXELS), BF16),
            pltpu.VMEM((BANDS, 2, QUARTER, MID), BF16),
            pltpu.VMEM((BANDS, 2, QUARTER, MID), BF16),
            pltpu.VMEM((BANDS, SHARE, PIXELS), BF16),
            pltpu.VMEM((BANDS, SHARE, PIXELS), BF16),
            pltpu.VMEM((len(OFFSETS), QUARTER, MID), BF16),
            pltpu.VMEM((len(OFFSETS), QUARTER, MID), BF16),
            pltpu.VMEM((BANDS, SHARE, QUARTER), F32),
            pltpu.SemaphoreType.DMA((2,)),
            pltpu.SemaphoreType.DMA((2,)),
            pltpu.SemaphoreType.DMA((2, len(OFFSETS))),
            pltpu.SemaphoreType.DMA((2, len(OFFSETS))),
            pltpu.SemaphoreType.DMA((4, BANDS)),
            pltpu.SemaphoreType.DMA((4, BANDS)),
        ],
        compiler_params=pltpu.CompilerParams(collective_id=1, has_side_effects=True),
    )(start, count, frames, conv, proj, grad)


def shards(frames, conv_weight, proj_weight, band_start, band_count, pyramid_grad):
    target, source, summed, wides = fetch(
        band_start, band_count, jnp.swapaxes(frames, 2, 3), conv_weight, proj_weight, jnp.swapaxes(pyramid_grad, 3, 4)
    )
    pyramid, source_share, target_share = tiles(
        band_count, source, target.reshape(2, PIXELS, MID), proj_weight, summed, wides
    )
    return jnp.swapaxes(pyramid, 3, 4), jnp.swapaxes(source_share, 1, 2), jnp.swapaxes(target_share, 1, 2)


def solution(mesh):
    in_specs = (
        P(None, "rows", None, None),
        P(),
        P(),
        P("rows"),
        P("rows"),
        P("rows", None, "band", None, None),
    )
    out_specs = (
        P("rows", None, "band", None, None),
        P("rows", None, "band"),
        P("rows", None, "band"),
    )
    return jax.shard_map(shards, mesh=mesh, in_specs=in_specs, out_specs=out_specs, check_vma=False)
```

time: 61.8 us -> 45.2 us (0.73)
  Pallas kernels: 59.6 us -> 43.1 us
    pallas_call x3 -> x1, Pallas kernels: 53 us -> 39.2 us  [fetch(): pl.pallas_call(fetch_kernel, in_specs=[smem, smem, vmem, vmem, vmem, vmem...]
    pallas_call x1, Pallas kernels: 6.59 us -> 3.93 us  [tiles(): pl.pallas_call(tile_kernel, grid=(2,), in_specs=[pl.BlockSpec(memory_spac...]
where the time goes in v4:
time: 45.2 us; the launch traced here: 45 us
  Pallas kernels  43.1 us (95%)
  between operations  1.93 us (4%)
    pallas_call x1, Pallas kernels, fetch(): pl.pallas_call(fetch_kernel, in_specs=[smem, smem, vmem, vmem, vmem, vmem...  39.2 us
    pallas_call x1, Pallas kernels, tiles(): pl.pallas_call(tile_kernel, grid=(2,), in_specs=[pl.BlockSpec(memory_spac...  3.93 us

profile of v4, /device:TPU:1, one launch (start us, length us, event | category | flops | bytes accessed | tf_op | source)
XLA Modules:
  0.0 45.0 jit_solution(7086719092121789306)
XLA Ops:
  1.9 39.2 %shard_map.85 = (bf16[2,4,128,128]{3,2,1,0:T(8,128)(2,1)}, bf16[512,128]{1,0:T(8,128)(2,1)}, f32[2,64,256]{2,1,0:T(8,128)}, f32[4,64,128]{2,1,0:T(8,128)}) custom-call(s32[1]{0:T(128)S(6)} %copy.9.start_ref, s32[1]{0:T(128)S(6)} %copy.10.count_ref, bf16[2,4,96,512]{3,2,1,0:T(8,128)(2,1)} %bitcast.7, bf16[3,3,96,128]{3,2,1,0:T(8,128)(2,1)} %conv_ref.1, ...), custom_call_target="tpu_custom_call" | custom-call | tf_op jit(solution)/shard_map/pallas_call | solution.py:250
  41.1 3.9 %shard_map.86 = (bf16[1,2,1,960,512]{4,3,2,1,0:T(8,128)(2,1)}, f32[2,64,256]{2,1,0:T(8,128)}, f32[2,64,256]{2,1,0:T(8,128)}) custom-call(s32[1]{0:T(128)S(6)} %copy.10.count_ref, bf16[512,128]{1,0:T(8,128)(2,1)} %get-tuple-element.10.source_ref, bf16[2,512,128]{2,1,0:T(8,128)(2,1)} %bitcast.8, bf16[128,256]{1,0:T(8,128)(2,1)} %proj_ref.3, ...), custom_call_target="tpu_custom_call" | custom-call | tf_op jit(solution)/shard_map/pallas_call | solution.py:66
